TPU v7x, 32 devices: a whole 2x2x4 slice. The times are simulated.
32 devices in a mesh: group: 16 (over z, x, core), tensor: 2 (over y).
Axes of the slice: x: 2, y: 2, z: 4, core: 2. Of those that a mesh axis runs over, the one named last changes fastest.
Arguments:
- prompt_cache: bfloat16 [2, 65536, 1024], P(None, ('group', 'tensor')), may hold values from -6 to 6
- queries: bfloat16 [32, 64, 8192], P('group', None, 'tensor'), may hold values from -10 to 10
- new_cache: bfloat16 [2, 32, 64, 1024], P(None, 'group', None, 'tensor'), may hold values from -6 to 6
- offsets: int32 [16, 2], P('group'), may hold values from 0 to 3
- lengths: int32 [16], P('group'), may hold values from 64 to 4096
- block_table: int32 [16, 32], P('group'), may hold values from 0 to 31, each once within a row
Outputs:
- attention: bfloat16 [32, 64, 8192], P('group', None, 'tensor')
Inputs may be any that keep to these rules, and one draw needn't show every extreme that they name: Each row of block_table names each of the 32 stored blocks of its prompt once.
All inputs are finite; a program needn't handle non-finite values.
Results may differ from a plain program's by a relative error of at most 0.0095.
Values may be sent and summed in bfloat16 or wider, within the bound.
A program may use at most 128 MiB of HBM per device.

v0:
```python
from functools import partial

import jax
import jax.numpy as jnp
from jax import lax
from jax.experimental import pallas as pl
from jax.experimental.pallas import tpu as pltpu
from jax.sharding import PartitionSpec as P


HD = 128
BLOCK = 128
STEPS = 4
REACH = 4
TEAM = 2
LADDER = (16, 8, 4)
PIECE = 128
LOG2E = 1.4426950408889634
AXES = ("group", "tensor")

masked_score = -1e30


def prompt_kernel(sub, members, links, cap, group_size, stage, info_ref, *refs):
    count = len(links)
    kv_refs = refs[: sub * members]
    query_refs = refs[sub * members : sub * members + count]
    out_refs = refs[sub * members + count : sub * members + 2 * count]
    keys, values, asked, answers, sems, query_sems, out_sems = refs[sub * members + 2 * count :]
    tokens = kv_refs[0].shape[1]
    rows = asked.shape[1]
    width = group_size * HD
    factor = HD ** -0.5 * LOG2E
    blocks = members * tokens // BLOCK
    per_piece = max(1, PIECE // rows)
    pieces = group_size // per_piece
    piece = per_piece * rows

    copies = []
    for j in range(sub):
        for r in range(members):
            source = kv_refs[j * members + r]
            for part, target in ((0, keys), (1, values)):
                copy = pltpu.make_async_copy(
                    source.at[part],
                    target.at[j, pl.ds(r * tokens, tokens), :],
                    sems.at[j, r, part],
                )
                copy.start()
                copies.append(copy)
    for n in range(count):
        copy = pltpu.make_async_copy(
            query_refs[n].at[:, :, pl.ds(stage * width, width)],
            asked.at[pl.ds(n * cap, cap)],
            query_sems.at[n],
        )
        copy.start()
        copies.append(copy)
    for copy in copies:
        copy.wait()

    lane = lax.broadcasted_iota(jnp.int32, (rows, HD), 1)

    def one(c, carry):
        j = info_ref[sub * (blocks + 1) + c]

        @pl.when(j >= 0)
        def _():
            base = j * (blocks + 1)
            length = info_ref[base]
            query = jnp.concatenate(
                [asked[c, :, g * HD : (g + 1) * HD] for g in range(group_size)], axis=0
            )

            def step(gather, masked, i, state):
                chunk = gather * BLOCK
                key_parts, value_parts = [], []
                for u in range(gather):
                    where = info_ref[base + 1 + i * gather + u]
                    rows_at = pl.ds(pl.multiple_of(where * BLOCK, BLOCK), BLOCK)
                    key_parts.append(keys[j, rows_at, :])
                    value_parts.append(values[j, rows_at, :])
                key = jnp.concatenate(key_parts, axis=0)
                value = jnp.concatenate(value_parts, axis=0)
                value = jnp.concatenate([value, jnp.ones_like(value)], axis=1)
                all_scores = [
                    lax.dot_general(
                        query[a * piece : (a + 1) * piece], key, (((1,), (1,)), ((), ())),
                        preferred_element_type=jnp.float32,
                    )
                    for a in range(pieces)
                ]
                result = []
                for scores, (peak, acc) in zip(all_scores, state):
                    if masked:
                        token = lax.broadcasted_iota(jnp.int32, (piece, chunk), 1)
                        scores = jnp.where(token < length - i * chunk, scores, masked_score)
                    new_peak = jnp.maximum(peak, jnp.max(scores, axis=1, keepdims=True))
                    weights = jnp.exp2(scores * factor - new_peak * factor)
                    decay = jnp.exp2(peak * factor - new_peak * factor)
                    acc = acc * decay + lax.dot_general(
                        weights.astype(jnp.bfloat16), value, (((1,), (0,)), ((), ())),
                        preferred_element_type=jnp.float32,
                    )
                    result.append((new_peak, acc))
                return tuple(result)

            state = tuple(
                (
                    jnp.full((piece, 1), masked_score, jnp.float32),
                    jnp.zeros((piece, 2 * HD), jnp.float32),
                )
                for _ in range(pieces)
            )
            done = 0
            for gather in LADDER:
                if blocks % gather:
                    continue
                chunk = gather * BLOCK
                start = done // chunk
                state = lax.fori_loop(
                    start, length // chunk, partial(step, gather, False), state
                )
                done = length // chunk * chunk
            start = done // chunk
            state = lax.fori_loop(
                start, (length + chunk - 1) // chunk, partial(step, gather, True), state
            )
            stats = jnp.zeros((rows, HD), jnp.float32)
            for a in range(pieces):
                peak, acc = state[a]
                total = acc[:, HD:]
                result = (acc[:, :HD] / total).astype(jnp.bfloat16)
                level = peak * HD ** -0.5 + jnp.log(total)
                for u in range(per_piece):
                    g = a * per_piece + u
                    span = slice(u * rows, (u + 1) * rows)
                    answers[c, :, g * HD : (g + 1) * HD] = result[span]
                    high = level[span].astype(jnp.bfloat16).astype(jnp.float32)
                    low = level[span] - high
                    stats = jnp.where(lane == g, high, stats)
                    stats = jnp.where(lane == group_size + g, low, stats)
            answers[c, :, group_size * HD :] = stats.astype(jnp.bfloat16)

        return carry

    lax.fori_loop(0, count * cap, one, 0)

    copies = []
    for n in range(count):
        copy = pltpu.make_async_copy(answers.at[pl.ds(n * cap, cap)], out_refs[n], out_sems.at[n])
        copy.start()
        copies.append(copy)
    for copy in copies:
        copy.wait()


def prompt_call(sub, members, links, cap, group_size, stage, info, chunks, fetched):
    rows = fetched[0].shape[1]
    tokens = chunks[0].shape[1]
    width = group_size * HD
    count = len(links)
    any_spec = pl.BlockSpec(memory_space=pl.ANY)
    return pl.pallas_call(
        partial(prompt_kernel, sub, members, links, cap, group_size, stage),
        grid_spec=pltpu.PrefetchScalarGridSpec(
            num_scalar_prefetch=1,
            grid=(1,),
            in_specs=[any_spec] * (len(chunks) + count),
            out_specs=[any_spec] * count,
            scratch_shapes=[
                pltpu.VMEM((sub, members * tokens, HD), jnp.bfloat16),
                pltpu.VMEM((sub, members * tokens, HD), jnp.bfloat16),
                pltpu.VMEM((count * cap, rows, width), jnp.bfloat16),
                pltpu.VMEM((count * cap, rows, width + HD), jnp.bfloat16),
                pltpu.SemaphoreType.DMA((sub, members, 2)),
                pltpu.SemaphoreType.DMA((count,)),
                pltpu.SemaphoreType.DMA((count,)),
            ],
        ),
        out_shape=[jax.ShapeDtypeStruct((cap, rows, width + HD), jnp.bfloat16)] * count,
        compiler_params=pltpu.CompilerParams(vmem_limit_bytes=40 * 1024 * 1024),
        cost_estimate=pl.CostEstimate(
            flops=cap * rows * width * members * tokens * 4 * sub,
            bytes_accessed=sub * members * tokens * HD * 4,
            transcendentals=cap * rows * group_size * members * tokens,
        ),
        name="prompt_attention",
    )(info, *chunks, *fetched)


def merge_kernel(sub, heads, h, links, cap, group_size, info_ref, *refs):
    count = len(links)
    query_ref, new_ref = refs[:2]
    result_refs = refs[2 : 2 + count]
    out_ref, buffer, sems = refs[-3:]
    rows = query_ref.shape[1]
    width = group_size * HD
    row_at = lax.broadcasted_iota(jnp.int32, (rows, rows), 0)
    token_at = lax.broadcasted_iota(jnp.int32, (rows, rows), 1)
    visible = (row_at // STEPS == token_at // STEPS) & (token_at <= row_at)
    visible = jnp.concatenate([visible.astype(jnp.int32)] * group_size, axis=0) > 0

    copies = []
    for i in range(sub):
        head = info_ref[cap + i] * heads + h
        columns = pl.ds(pl.multiple_of(head * width, width), width)
        new_columns = pl.ds(pl.multiple_of(head * HD, HD), HD)
        for c in range(cap):
            served = info_ref[c]
            raw = query_ref[c, :, columns]
            query = jnp.concatenate(
                [raw[:, g * HD : (g + 1) * HD] for g in range(group_size)], axis=0
            )
            key = new_ref[0, c, :, new_columns]
            value = new_ref[1, c, :, new_columns]
            scores = lax.dot_general(
                query, key, (((1,), (1,)), ((), ())), preferred_element_type=jnp.float32
            ) * HD ** -0.5
            scores = jnp.where(visible, scores, masked_score)
            peak = jnp.max(scores, axis=1, keepdims=True)
            weights = jnp.exp(scores - peak)
            total = jnp.sum(weights, axis=1, keepdims=True)
            own = lax.dot_general(
                weights.astype(jnp.bfloat16), value, (((1,), (0,)), ((), ())),
                preferred_element_type=jnp.float32,
            )
            chosen = None
            for n, (s, index) in enumerate(links):
                if index != i:
                    continue
                block = result_refs[n][c]
                chosen = block if chosen is None else jnp.where(served == s, block, chosen)
            stats = chosen[:, width:].astype(jnp.float32)
            pieces = []
            for g in range(group_size):
                span = slice(g * rows, (g + 1) * rows)
                level = stats[:, g : g + 1] + stats[:, group_size + g : group_size + g + 1]
                highest = jnp.maximum(level, peak[span])
                scale = jnp.exp(level - highest)
                own_scale = jnp.exp(peak[span] - highest)
                inverse = 1.0 / (scale + total[span] * own_scale)
                part = chosen[:, g * HD : (g + 1) * HD].astype(jnp.float32)
                pieces.append((scale * inverse) * part + (own_scale * inverse) * own[span])
            buffer[i, c] = jnp.concatenate(pieces, axis=1).astype(jnp.bfloat16)
            copy = pltpu.make_async_copy(buffer.at[i, c], out_ref.at[c, :, columns], sems.at[i, c])
            copy.start()
            copies.append(copy)
    for copy in copies:
        copy.wait()


def merge_call(sub, heads, h, links, cap, group_size, info, queries, new_cache, results, earlier):
    full = lambda shape: pl.BlockSpec(shape, lambda i, info: (0,) * len(shape))
    any_spec = pl.BlockSpec(memory_space=pl.ANY)
    rows = queries.shape[1]
    operands = [queries, new_cache, *results]
    specs = [full(x.shape) for x in operands]
    aliases = {}
    if earlier is not None:
        aliases = {1 + len(operands): 0}
        operands.append(earlier)
        specs.append(any_spec)
    return pl.pallas_call(
        partial(merge_kernel, sub, heads, h, links, cap, group_size),
        grid_spec=pltpu.PrefetchScalarGridSpec(
            num_scalar_prefetch=1,
            grid=(1,),
            in_specs=specs,
            out_specs=any_spec,
            scratch_shapes=[
                pltpu.VMEM((sub, cap, rows, group_size * HD), jnp.bfloat16),
                pltpu.SemaphoreType.DMA((sub, cap)),
            ],
        ),
        out_shape=jax.ShapeDtypeStruct(queries.shape, jnp.bfloat16),
        input_output_aliases=aliases,
        compiler_params=pltpu.CompilerParams(vmem_limit_bytes=40 * 1024 * 1024),
        cost_estimate=pl.CostEstimate(
            flops=sub * cap * rows * rows * group_size * HD * 4,
            bytes_accessed=8 * rows * cap * group_size * HD * sub,
            transcendentals=sub * cap * rows * rows * group_size,
        ),
        name="merge",
    )(info, *operands)


def shards(prompt_cache, queries, new_cache, offsets, lengths, block_table):
    members = lax.axis_size("tensor")
    groups = lax.axis_size("group")
    cap = queries.shape[0]
    tokens = prompt_cache.shape[1]
    kv_local = prompt_cache.shape[2] // HD // members
    group_size = queries.shape[2] // (kv_local * HD)
    width = group_size * HD
    sub = TEAM if kv_local % TEAM == 0 and groups % TEAM == 0 else 1
    heads = kv_local // sub
    teams = groups // sub
    me = lax.axis_index("group").astype(jnp.int32)
    member = lax.axis_index("tensor").astype(jnp.int32)
    seat = me % sub

    def device(team_at, seat_at, member_at):
        return ((team_at % teams) * sub + seat_at) * members + member_at % members

    def reaches(s, seat_at):
        return s * sub + seat_at - (sub - 1) <= REACH - 1

    links = []
    for s in range(REACH):
        if reaches(s, 0):
            links += [(s, i) for i in range(sub)]

    def pairs_of(s, i, back):
        pairs = []
        for a in range(teams):
            for b in range(sub):
                if reaches(s, b ^ i):
                    for m in range(members):
                        pair = (device(a + s, b ^ i, m), device(a, b, m))
                        pairs.append(pair[::-1] if back else pair)
        return pairs

    def to_prompt(value_of, s, i):
        value = value_of(seat ^ i)
        if s == 0 and i == 0:
            return value
        return lax.ppermute(value, AXES, pairs_of(s, i, False))

    meta = jnp.concatenate(
        [offsets.reshape(-1), lengths.reshape(-1), block_table.reshape(-1)]
    ).astype(jnp.int32)[None]
    metas = [to_prompt(lambda other: meta, s, i)[0] for s, i in links]

    def query_part(other):
        return lax.dynamic_slice_in_dim(queries, other * heads * width, heads * width, 2)

    def cache_slice(cache, j, r, h):
        other = ((member + r) % members) * kv_local + (seat ^ j) * heads + h
        return lax.dynamic_slice_in_dim(cache, other * HD, HD, 2)

    def cache_part(part, j, r):
        if j == 0 and r == 0:
            return part
        pairs = [
            (device(a, b, m), device(a, b ^ j, m + r))
            for a in range(teams) for b in range(sub) for m in range(members)
        ]
        return lax.ppermute(part, AXES, pairs)

    fetched = [to_prompt(query_part, s, i) for s, i in links]
    seats_of = [(j, r) for j in range(sub) for r in range(members)]
    stage_chunks = []
    cache = prompt_cache
    for h in range(heads):
        slices = [cache_slice(cache, j, r, h) for j, r in seats_of]
        cache, slices = lax.optimization_barrier((cache, slices))
        stage_chunks.append([cache_part(p, j, r) for p, (j, r) in zip(slices, seats_of)])

    per_member = tokens // BLOCK
    rows_info = []
    for j in range(sub):
        row = metas[j]
        table = row[cap + 1 :]
        order = ((member - table // per_member) % members) * per_member + table % per_member
        rows_info += [row[cap : cap + 1], order]
    wanted = []
    for n, (s, i) in enumerate(links):
        decode = (s * sub + (seat ^ i))
        prompt = decode - metas[n][:cap]
        here = (prompt >= 0) & (prompt < sub) & reaches(s, seat ^ i)
        wanted.append(jnp.where(here, prompt ^ seat, -1))
    info = jnp.concatenate(rows_info + wanted).astype(jnp.int32)

    own_offset = offsets.reshape(-1).astype(jnp.int32)
    served = jnp.where(own_offset <= seat, 0, (own_offset - seat + sub - 1) // sub)
    seats = jnp.stack([seat ^ i for i in range(sub)])
    merge_info = jnp.concatenate([served, seats]).astype(jnp.int32)
    output = None
    for h in range(heads):
        parts = prompt_call(
            sub, members, links, cap, group_size, h, info, stage_chunks[h], fetched
        )
        results = []
        for n, (s, i) in enumerate(links):
            if s == 0 and i == 0:
                results.append(parts[n])
            else:
                results.append(lax.ppermute(parts[n], AXES, pairs_of(s, i, True)))
        output = merge_call(
            sub, heads, h, links, cap, group_size, merge_info, queries, new_cache, results, output
        )
    return output


def solution(mesh):
    in_specs = (
        P(None, ("group", "tensor"), None),
        P("group", None, "tensor"),
        P(None, "group", None, "tensor"),
        P("group", None),
        P("group"),
        P("group", None),
    )
    out_specs = P("group", None, "tensor")

    return jax.shard_map(shards, mesh=mesh, in_specs=in_specs, out_specs=out_specs, check_vma=False)
```

profile of v0, /device:TPU:18, one launch (start us, length us, event | category | flops | bytes accessed | tf_op | source)
XLA Modules:
  0.0 169.3 jit_solution(10676477560589269031)
XLA Ops:
  0.0 2.1 %constant_dynamic-slice_fusion = (bf16[2,64,2048]{2,1,0:T(8,128)(2,1)}, bf16[2,64,2048]{2,1,0:T(8,128)(2,1)S(1)}) fusion(bf16[2,64,4096]{2,1,0:T(8,128)(2,1)} %refs_0_.3, s32[]{:T(128)S(6)} %select_n.141, s32[]{:T(128)S(6)} %select_n.140), kind=kLoop, calls=%fused_computation | loop fusion | bytes 2097160 | tf_op jit(solution)/shard_map/dynamic_slice | solution.py:336
  2.1 1.8 %collective-permute-start.12 = (bf16[2,64,2048]{2,1,0:T(8,128)(2,1)}, bf16[2,64,2048]{2,1,0:T(8,128)(2,1)S(1)}, u32[]{:S(2)}, u32[]{:S(2)}) collective-permute-start(bf16[2,64,2048]{2,1,0:T(8,128)(2,1)} %get-tuple-element.55), channel_id=1, source_target_pairs={{8,2},{9,3},{12,6},{13,7},{16,10},{17,11},{20,14},{21,15},{24,18},... | collective-permute-start | bytes 1572872 | tf_op jit(solution)/shard_map/ppermute | solution.py:328
  6.1 1.9 %collective-permute-start.4 = (s32[1,35]{1,0:T(1,128)S(1)}, s32[1,35]{1,0:T(1,128)S(1)}, u32[]{:S(2)}, u32[]{:S(2)}) collective-permute-start(s32[1,35]{1,0:T(1,128)S(1)} %add_bitcast_fusion), channel_id=1, source_target_pairs={{8,2},{9,3},{12,6},{13,7},{16,10},{17,11},{20,14},{21,15},{24,18},... | collective-permute-start | bytes 428 | tf_op jit(solution)/shard_map/ppermute | solution.py:328
  8.0 4.1 %constant_dynamic-slice_fusion.6 = (bf16[2,2048,128]{2,1,0:T(8,128)(2,1)}, bf16[2,2048,128]{2,1,0:T(8,128)(2,1)}, bf16[2,2048,128]{2,1,0:T(8,128)(2,1)}, bf16[2,2048,128]{2,1,0:T(8,128)(2,1)S(1)}) fusion(bf16[2,2048,1024]{2,1,0:T(8,128)(2,1)} %param.6, s32[]{:T(128)S(6)} %select_n.135, s32[]{:T(128)S(6)} %select_n.134, s32[]{:T(128)S(6)} %select_n.133, ...), kind=kLoop, calls=%fused_computation.6 | loop fusion | bytes 8388624 | tf_op jit(solution)/shard_map/dynamic_slice | solution.py:340
  12.1 1.6 collective-permute-start.18
  13.7 4.0 %constant_dynamic-slice_fusion.2 = (bf16[2,2048,128]{2,1,0:T(8,128)(2,1)}, bf16[2,2048,128]{2,1,0:T(8,128)(2,1)}, bf16[2,2048,128]{2,1,0:T(8,128)(2,1)}, bf16[2,2048,128]{2,1,0:T(8,128)(2,1)S(1)}) fusion(bf16[2,2048,1024]{2,1,0:T(8,128)(2,1)} %param.6, s32[]{:T(128)S(6)} %select_n.139, s32[]{:T(128)S(6)} %select_n.138, s32[]{:T(128)S(6)} %select_n.137, ...), kind=kLoop, calls=%fused_computation.2 | loop fusion | bytes 8388624 | tf_op jit(solution)/shard_map/dynamic_slice | solution.py:340
  17.7 5.5 %collective-permute-start.3 = (s32[1,35]{1,0:T(1,128)S(1)}, s32[1,35]{1,0:T(1,128)S(1)}, u32[]{:S(2)}, u32[]{:S(2)}) collective-permute-start(s32[1,35]{1,0:T(1,128)S(1)} %add_bitcast_fusion), channel_id=1, source_target_pairs={{8,0},{9,1},{12,4},{13,5},{16,8},{17,9},{20,12},{21,13},{24,16},{2... | collective-permute-start | bytes 428 | tf_op jit(solution)/shard_map/ppermute | solution.py:328
  23.2 1.3 collective-permute-done.3
  25.2 3.7 %collective-permute-done.2 = s32[1,35]{1,0:T(1,128)S(1)} collective-permute-done((s32[1,35]{1,0:T(1,128)S(1)}, s32[1,35]{1,0:T(1,128)S(1)}, u32[]{:S(2)}, u32[]{:S(2)}) %collective-permute-start.2) | collective-permute-done | bytes 172 | tf_op jit(solution)/shard_map/ppermute | solution.py:328
  28.8 2.3 %collective-permute-start.1 = (s32[1,35]{1,0:T(1,128)S(1)}, s32[1,35]{1,0:T(1,128)S(1)}, u32[]{:S(2)}, u32[]{:S(2)}) collective-permute-start(s32[1,35]{1,0:T(1,128)S(1)} %add_bitcast_fusion), channel_id=1, source_target_pairs={{4,0},{5,1},{6,2},{7,3},{8,4},{9,5},{10,6},{11,7},{12,8},{13,9},{1... | collective-permute-start | bytes 428 | tf_op jit(solution)/shard_map/ppermute | solution.py:328
  31.1 4.4 %collective-permute-done.1 = s32[1,35]{1,0:T(1,128)S(1)} collective-permute-done((s32[1,35]{1,0:T(1,128)S(1)}, s32[1,35]{1,0:T(1,128)S(1)}, u32[]{:S(2)}, u32[]{:S(2)}) %collective-permute-start.1) | collective-permute-done | bytes 172 | tf_op jit(solution)/shard_map/ppermute | solution.py:328
  36.6 1.9 %collective-permute-start.11 = (bf16[2,64,2048]{2,1,0:T(8,128)(2,1)S(1)}, bf16[2,64,2048]{2,1,0:T(8,128)(2,1)S(1)}, u32[]{:S(2)}, u32[]{:S(2)}) collective-permute-start(bf16[2,64,2048]{2,1,0:T(8,128)(2,1)S(1)} %get-tuple-element.56.refs_4_), channel_id=1, source_target_pairs={{8,0},{9,1},{12,4},{13,5},{16,8},{17,9},{20,12},{21,13},{24,16},{2... | collective-permute-start | bytes 1572872 | tf_op jit(solution)/shard_map/ppermute | solution.py:328
  40.3 1.6 collective-permute-start.20
  42.0 6.9 %collective-permute-done.11.refs_8_ = bf16[2,64,2048]{2,1,0:T(8,128)(2,1)S(1)} collective-permute-done((bf16[2,64,2048]{2,1,0:T(8,128)(2,1)S(1)}, bf16[2,64,2048]{2,1,0:T(8,128)(2,1)S(1)}, u32[]{:S(2)}, u32[]{:S(2)}) %collective-permute-start.11) | collective-permute-done | bytes 524320 | tf_op jit(solution)/shard_map/ppermute | solution.py:328
  49.7 1.5 collective-permute-start.5
  51.2 6.7 %collective-permute-done.9.refs_6_ = bf16[2,64,2048]{2,1,0:T(8,128)(2,1)S(1)} collective-permute-done((bf16[2,64,2048]{2,1,0:T(8,128)(2,1)S(1)}, bf16[2,64,2048]{2,1,0:T(8,128)(2,1)S(1)}, u32[]{:S(2)}, u32[]{:S(2)}) %collective-permute-start.9) | collective-permute-done | bytes 524320 | tf_op jit(solution)/shard_map/ppermute | solution.py:328
  58.7 1.6 collective-permute-start.7
  61.1 4.7 %collective-permute-done.20.refs_3_ = bf16[2,2048,128]{2,1,0:T(8,128)(2,1)} collective-permute-done((bf16[2,2048,128]{2,1,0:T(8,128)(2,1)}, bf16[2,2048,128]{2,1,0:T(8,128)(2,1)}, u32[]{:S(2)}, u32[]{:S(2)}) %collective-permute-start.20) | collective-permute-done | bytes 1048608 | tf_op jit(solution)/shard_map/ppermute | solution.py:349
  65.8 1.0 copy-done.3
  67.9 29.1 %prompt_attention.3 = (bf16[2,64,1152]{2,1,0:T(8,128)(2,1)S(1)}, bf16[2,64,1152]{2,1,0:T(8,128)(2,1)S(1)}, bf16[2,64,1152]{2,1,0:T(8,128)(2,1)S(1)}, bf16[2,64,1...) custom-call(s32[78]{0:T(128)S(1)} %concatenate.11.info_ref, ...), custom_call_target="tpu_custom_call" | custom-call | flops 4294967296 | bytes 4194304 | tf_op jit(solution)/shard_map/prompt_attention/pallas_call | solution.py:164
  97.9 1.9 %collective-permute-start.24 = (bf16[2,64,1152]{2,1,0:T(8,128)(2,1)S(1)}, bf16[2,64,1152]{2,1,0:T(8,128)(2,1)S(1)}, u32[]{:S(2)}, u32[]{:S(2)}) collective-permute-start(bf16[2,64,1152]{2,1,0:T(8,128)(2,1)S(1)} %get-tuple-element.45), channel_id=1, source_target_pairs={{0,8},{1,9},{4,12},{5,13},{8,16},{9,17},{12,20},{13,21},{16,24},{1... | collective-permute-start | bytes 884744 | tf_op jit(solution)/shard_map/ppermute | solution.py:389
  99.8 10.6 %collective-permute-done.7.refs_3_ = bf16[2,2048,128]{2,1,0:T(8,128)(2,1)} collective-permute-done((bf16[2,2048,128]{2,1,0:T(8,128)(2,1)}, bf16[2,2048,128]{2,1,0:T(8,128)(2,1)}, u32[]{:S(2)}, u32[]{:S(2)}) %collective-permute-start.7) | collective-permute-done | bytes 1048608 | tf_op jit(solution)/shard_map/ppermute | solution.py:349
  110.5 1.5 collective-permute-start.25
  112.0 29.1 %prompt_attention.2 = (bf16[2,64,1152]{2,1,0:T(8,128)(2,1)S(1)}, bf16[2,64,1152]{2,1,0:T(8,128)(2,1)S(1)}, bf16[2,64,1152]{2,1,0:T(8,128)(2,1)S(1)}, bf16[2,64,1...) custom-call(s32[78]{0:T(128)S(1)} %concatenate.11.info_ref, ...), custom_call_target="tpu_custom_call" | custom-call | flops 4294967296 | bytes 4194304 | tf_op jit(solution)/shard_map/prompt_attention/pallas_call | solution.py:164
  141.1 3.0 %collective-permute-start.13 = (bf16[2,64,1152]{2,1,0:T(8,128)(2,1)S(1)}, bf16[2,64,1152]{2,1,0:T(8,128)(2,1)S(1)}, u32[]{:S(2)}, u32[]{:S(2)}) collective-permute-start(bf16[2,64,1152]{2,1,0:T(8,128)(2,1)S(1)} %get-tuple-element.32), channel_id=1, source_target_pairs={{0,2},{1,3},{2,0},{3,1},{4,6},{5,7},{6,4},{7,5},{8,10},{9,11},{10,... | collective-permute-start | bytes 884744 | tf_op jit(solution)/shard_map/ppermute | solution.py:389
  144.2 1.9 %collective-permute-start.16 = (bf16[2,64,1152]{2,1,0:T(8,128)(2,1)S(1)}, bf16[2,64,1152]{2,1,0:T(8,128)(2,1)S(1)}, u32[]{:S(2)}, u32[]{:S(2)}) collective-permute-start(bf16[2,64,1152]{2,1,0:T(8,128)(2,1)S(1)} %get-tuple-element.35), channel_id=1, source_target_pairs={{0,8},{1,9},{4,12},{5,13},{8,16},{9,17},{12,20},{13,21},{16,24},{1... | collective-permute-start | bytes 884744 | tf_op jit(solution)/shard_map/ppermute | solution.py:389
  146.1 1.3 collective-permute-start.17
  147.5 3.3 %merge.2.refs_8_ = bf16[2,64,4096]{2,1,0:T(8,128)(2,1)} custom-call(s32[4]{0:T(128)S(1)} %pad_add_fusion.info_ref, bf16[2,64,4096]{2,1,0:T(8,128)(2,1)S(1)} %copy-done, bf16[2,2,64,512]{3,2,1,0:T(8,128)(2,1)S(1)} %copy-done.1, bf16[2,64,1152]{2,1,0:T(8,128)(2,1)S(1)} %get-tuple-element.41.refs_2_, bf16[2,64,1152]{2,1,0:T(8,128)(2,1)S(1)} %collective-permute-done.21.refs_3_, ...), custom_call_target="tpu_custom_call" | custom-call | flops 67108864 | bytes 2097152 | tf_op jit(solution)/shard_map/merge/pallas_call | solution.py:264
  150.9 3.1 %collective-permute-done.14.refs_4_ = bf16[2,64,1152]{2,1,0:T(8,128)(2,1)S(1)} collective-permute-done((bf16[2,64,1152]{2,1,0:T(8,128)(2,1)S(1)}, bf16[2,64,1152]{2,1,0:T(8,128)(2,1)S(1)}, u32[]{:S(2)}, u32[]{:S(2)}) %collective-permute-start.14) | collective-permute-done | bytes 294944 | tf_op jit(solution)/shard_map/ppermute | solution.py:389
  154.0 4.5 %collective-permute-done.15.refs_5_ = bf16[2,64,1152]{2,1,0:T(8,128)(2,1)S(1)} collective-permute-done((bf16[2,64,1152]{2,1,0:T(8,128)(2,1)S(1)}, bf16[2,64,1152]{2,1,0:T(8,128)(2,1)S(1)}, u32[]{:S(2)}, u32[]{:S(2)}) %collective-permute-start.15) | collective-permute-done | bytes 294944 | tf_op jit(solution)/shard_map/ppermute | solution.py:389
  158.5 7.2 %collective-permute-done.16.refs_6_ = bf16[2,64,1152]{2,1,0:T(8,128)(2,1)S(1)} collective-permute-done((bf16[2,64,1152]{2,1,0:T(8,128)(2,1)S(1)}, bf16[2,64,1152]{2,1,0:T(8,128)(2,1)S(1)}, u32[]{:S(2)}, u32[]{:S(2)}) %collective-permute-start.16) | collective-permute-done | bytes 294944 | tf_op jit(solution)/shard_map/ppermute | solution.py:389
  165.7 3.4 %merge.3 = bf16[2,64,4096]{2,1,0:T(8,128)(2,1)} custom-call(s32[4]{0:T(128)S(1)} %pad_add_fusion.info_ref, bf16[2,64,4096]{2,1,0:T(8,128)(2,1)S(1)} %copy-done, bf16[2,2,64,512]{3,2,1,0:T(8,128)(2,1)S(1)} %copy-done.1, bf16[2,64,1152]{2,1,0:T(8,128)(2,1)S(1)} %get-tuple-element.31.refs_2_, ...), custom_call_target="tpu_custom_call", output_to_operand_aliasing={{}: (9, {})} | custom-call | flops 67108864 | bytes 2097152 | tf_op jit(solution)/shard_map/merge/pallas_call | solution.py:264
  (59 shorter events, 9.5 us)
Async XLA Ops:
  0.0 13.7 %copy-start.8 = (s32[1,2]{1,0:T(1,128)S(1)}, s32[1,2]{1,0:T(1,128)}, u32[]{:S(2)}) copy-start(s32[1,2]{1,0:T(1,128)} %param.9) | copy-start | bytes 28
  0.0 13.7 %copy-start.9 = (s32[1,32]{1,0:T(1,128)S(1)}, s32[1,32]{1,0:T(1,128)}, u32[]{:S(2)}) copy-start(s32[1,32]{1,0:T(1,128)} %param.11) | copy-start | bytes 388
  2.1 36.4 %collective-permute-start.12 = (bf16[2,64,2048]{2,1,0:T(8,128)(2,1)}, bf16[2,64,2048]{2,1,0:T(8,128)(2,1)S(1)}, u32[]{:S(2)}, u32[]{:S(2)}) collective-permute-start(bf16[2,64,2048]{2,1,0:T(8,128)(2,1)} %get-tuple-element.55), channel_id=1, source_target_pairs={{8,2},{9,3},{12,6},{13,7},{16,10},{17,11},{20,14},{21,15},{24,18},... | collective-permute-start | bytes 1572872 | tf_op jit(solution)/shard_map/ppermute | solution.py:328
  3.9 36.4 %collective-permute-start.10 = (bf16[2,64,2048]{2,1,0:T(8,128)(2,1)}, bf16[2,64,2048]{2,1,0:T(8,128)(2,1)}, u32[]{:S(2)}, u32[]{:S(2)}) collective-permute-start(bf16[2,64,2048]{2,1,0:T(8,128)(2,1)} %get-tuple-element.55), channel_id=1, source_target_pairs={{6,0},{7,1},{4,2},{5,3},{10,4},{11,5},{8,6},{9,7},{14,8},{15,9},{1... | collective-permute-start | bytes 1572872 | tf_op jit(solution)/shard_map/ppermute | solution.py:328
  4.0 36.3 %collective-permute-start.8 = (bf16[2,64,2048]{2,1,0:T(8,128)(2,1)}, bf16[2,64,2048]{2,1,0:T(8,128)(2,1)}, u32[]{:S(2)}, u32[]{:S(2)}) collective-permute-start(bf16[2,64,2048]{2,1,0:T(8,128)(2,1)} %get-tuple-element.55), channel_id=1, source_target_pairs={{2,0},{3,1},{0,2},{1,3},{6,4},{7,5},{4,6},{5,7},{10,8},{11,9},{8,1... | collective-permute-start | bytes 1572872 | tf_op jit(solution)/shard_map/ppermute | solution.py:328
  6.1 11.7 %collective-permute-start.4 = (s32[1,35]{1,0:T(1,128)S(1)}, s32[1,35]{1,0:T(1,128)S(1)}, u32[]{:S(2)}, u32[]{:S(2)}) collective-permute-start(s32[1,35]{1,0:T(1,128)S(1)} %add_bitcast_fusion), channel_id=1, source_target_pairs={{8,2},{9,3},{12,6},{13,7},{16,10},{17,11},{20,14},{21,15},{24,18},... | collective-permute-start | bytes 428 | tf_op jit(solution)/shard_map/ppermute | solution.py:328
  12.1 46.7 %collective-permute-start.18 = (bf16[2,2048,128]{2,1,0:T(8,128)(2,1)}, bf16[2,2048,128]{2,1,0:T(8,128)(2,1)}, u32[]{:S(2)}, u32[]{:S(2)}) collective-permute-start(bf16[2,2048,128]{2,1,0:T(8,128)(2,1)} %get-tuple-element.38), channel_id=1, source_target_pairs={{0,1},{1,0},{2,3},{3,2},{4,5},{5,4},{6,7},{7,6},{8,9},{9,8},{10,11... | collective-permute-start | bytes 3145736 | tf_op jit(solution)/shard_map/ppermute | solution.py:349
  17.7 6.8 %collective-permute-start.3 = (s32[1,35]{1,0:T(1,128)S(1)}, s32[1,35]{1,0:T(1,128)S(1)}, u32[]{:S(2)}, u32[]{:S(2)}) collective-permute-start(s32[1,35]{1,0:T(1,128)S(1)} %add_bitcast_fusion), channel_id=1, source_target_pairs={{8,0},{9,1},{12,4},{13,5},{16,8},{17,9},{20,12},{21,13},{24,16},{2... | collective-permute-start | bytes 428 | tf_op jit(solution)/shard_map/ppermute | solution.py:328
  24.5 4.4 %collective-permute-start.2 = (s32[1,35]{1,0:T(1,128)S(1)}, s32[1,35]{1,0:T(1,128)S(1)}, u32[]{:S(2)}, u32[]{:S(2)}) collective-permute-start(s32[1,35]{1,0:T(1,128)S(1)} %add_bitcast_fusion), channel_id=1, source_target_pairs={{6,0},{7,1},{4,2},{5,3},{10,4},{11,5},{8,6},{9,7},{14,8},{15,9},{1... | collective-permute-start | bytes 428 | tf_op jit(solution)/shard_map/ppermute | solution.py:328
  28.8 6.6 %collective-permute-start.1 = (s32[1,35]{1,0:T(1,128)S(1)}, s32[1,35]{1,0:T(1,128)S(1)}, u32[]{:S(2)}, u32[]{:S(2)}) collective-permute-start(s32[1,35]{1,0:T(1,128)S(1)} %add_bitcast_fusion), channel_id=1, source_target_pairs={{4,0},{5,1},{6,2},{7,3},{8,4},{9,5},{10,6},{11,7},{12,8},{13,9},{1... | collective-permute-start | bytes 428 | tf_op jit(solution)/shard_map/ppermute | solution.py:328
  35.5 1.2 collective-permute-start
  36.6 12.2 %collective-permute-start.11 = (bf16[2,64,2048]{2,1,0:T(8,128)(2,1)S(1)}, bf16[2,64,2048]{2,1,0:T(8,128)(2,1)S(1)}, u32[]{:S(2)}, u32[]{:S(2)}) collective-permute-start(bf16[2,64,2048]{2,1,0:T(8,128)(2,1)S(1)} %get-tuple-element.56.refs_4_), channel_id=1, source_target_pairs={{8,0},{9,1},{12,4},{13,5},{16,8},{17,9},{20,12},{21,13},{24,16},{2... | collective-permute-start | bytes 1572872 | tf_op jit(solution)/shard_map/ppermute | solution.py:328
  38.6 19.3 %collective-permute-start.9 = (bf16[2,64,2048]{2,1,0:T(8,128)(2,1)S(1)}, bf16[2,64,2048]{2,1,0:T(8,128)(2,1)S(1)}, u32[]{:S(2)}, u32[]{:S(2)}) collective-permute-start(bf16[2,64,2048]{2,1,0:T(8,128)(2,1)S(1)} %get-tuple-element.56.refs_4_), channel_id=1, source_target_pairs={{4,0},{5,1},{6,2},{7,3},{8,4},{9,5},{10,6},{11,7},{12,8},{13,9},{1... | collective-permute-start | bytes 1572872 | tf_op jit(solution)/shard_map/ppermute | solution.py:328
  40.3 20.8 %collective-permute-start.19 = (bf16[2,2048,128]{2,1,0:T(8,128)(2,1)}, bf16[2,2048,128]{2,1,0:T(8,128)(2,1)}, u32[]{:S(2)}, u32[]{:S(2)}) collective-permute-start(bf16[2,2048,128]{2,1,0:T(8,128)(2,1)} %get-tuple-element.39), channel_id=1, source_target_pairs={{0,2},{1,3},{2,0},{3,1},{4,6},{5,7},{6,4},{7,5},{8,10},{9,11},{10,... | collective-permute-start | bytes 3145736 | tf_op jit(solution)/shard_map/ppermute | solution.py:349
  40.3 25.5 %collective-permute-start.20 = (bf16[2,2048,128]{2,1,0:T(8,128)(2,1)}, bf16[2,2048,128]{2,1,0:T(8,128)(2,1)}, u32[]{:S(2)}, u32[]{:S(2)}) collective-permute-start(bf16[2,2048,128]{2,1,0:T(8,128)(2,1)} %get-tuple-element.40), channel_id=1, source_target_pairs={{0,3},{1,2},{2,1},{3,0},{4,7},{5,6},{6,5},{7,4},{8,11},{9,10},{10,... | collective-permute-start | bytes 3145736 | tf_op jit(solution)/shard_map/ppermute | solution.py:349
  49.7 48.2 %collective-permute-start.5 = (bf16[2,2048,128]{2,1,0:T(8,128)(2,1)}, bf16[2,2048,128]{2,1,0:T(8,128)(2,1)}, u32[]{:S(2)}, u32[]{:S(2)}) collective-permute-start(bf16[2,2048,128]{2,1,0:T(8,128)(2,1)} %get-tuple-element.28), channel_id=1, source_target_pairs={{0,1},{1,0},{2,3},{3,2},{4,5},{5,4},{6,7},{7,6},{8,9},{9,8},{10,11... | collective-permute-start | bytes 3145736 | tf_op jit(solution)/shard_map/ppermute | solution.py:349
  58.7 39.2 %collective-permute-start.6 = (bf16[2,2048,128]{2,1,0:T(8,128)(2,1)}, bf16[2,2048,128]{2,1,0:T(8,128)(2,1)}, u32[]{:S(2)}, u32[]{:S(2)}) collective-permute-start(bf16[2,2048,128]{2,1,0:T(8,128)(2,1)} %get-tuple-element.29), channel_id=1, source_target_pairs={{0,2},{1,3},{2,0},{3,1},{4,6},{5,7},{6,4},{7,5},{8,10},{9,11},{10,... | collective-permute-start | bytes 3145736 | tf_op jit(solution)/shard_map/ppermute | solution.py:349
  58.7 51.7 %collective-permute-start.7 = (bf16[2,2048,128]{2,1,0:T(8,128)(2,1)}, bf16[2,2048,128]{2,1,0:T(8,128)(2,1)}, u32[]{:S(2)}, u32[]{:S(2)}) collective-permute-start(bf16[2,2048,128]{2,1,0:T(8,128)(2,1)} %get-tuple-element.30), channel_id=1, source_target_pairs={{0,3},{1,2},{2,1},{3,0},{4,7},{5,6},{6,5},{7,4},{8,11},{9,10},{10,... | collective-permute-start | bytes 3145736 | tf_op jit(solution)/shard_map/ppermute | solution.py:349
  67.9 44.0 %copy-start.4 = (bf16[2,64,2048]{2,1,0:T(8,128)(2,1)S(1)}, bf16[2,64,2048]{2,1,0:T(8,128)(2,1)}, u32[]{:S(2)}) copy-start(bf16[2,64,2048]{2,1,0:T(8,128)(2,1)} %copy-done.2) | copy-start | bytes 1572868
  67.9 44.1 %copy-start.7 = (bf16[2,64,2048]{2,1,0:T(8,128)(2,1)S(1)}, bf16[2,64,2048]{2,1,0:T(8,128)(2,1)}, u32[]{:S(2)}) copy-start(bf16[2,64,2048]{2,1,0:T(8,128)(2,1)} %copy-done.5) | copy-start | bytes 1572868
  97.0 50.5 %copy-start = (bf16[2,64,4096]{2,1,0:T(8,128)(2,1)S(1)}, bf16[2,64,4096]{2,1,0:T(8,128)(2,1)}, u32[]{:S(2)}) copy-start(bf16[2,64,4096]{2,1,0:T(8,128)(2,1)} %refs_0_.3) | copy-start | bytes 3145732
  97.0 50.5 %copy-start.1 = (bf16[2,2,64,512]{3,2,1,0:T(8,128)(2,1)S(1)}, bf16[2,2,64,512]{3,2,1,0:T(8,128)(2,1)}, u32[]{:S(2)}) copy-start(bf16[2,2,64,512]{3,2,1,0:T(8,128)(2,1)} %refs_1_.3) | copy-start | bytes 786436
  97.0 44.1 %collective-permute-start.21 = (bf16[2,64,1152]{2,1,0:T(8,128)(2,1)S(1)}, bf16[2,64,1152]{2,1,0:T(8,128)(2,1)S(1)}, u32[]{:S(2)}, u32[]{:S(2)}) collective-permute-start(bf16[2,64,1152]{2,1,0:T(8,128)(2,1)S(1)} %get-tuple-element.42), channel_id=1, source_target_pairs={{0,2},{1,3},{2,0},{3,1},{4,6},{5,7},{6,4},{7,5},{8,10},{9,11},{10,... | collective-permute-start | bytes 884744 | tf_op jit(solution)/shard_map/ppermute | solution.py:389
  97.9 46.2 %collective-permute-start.22 = (bf16[2,64,1152]{2,1,0:T(8,128)(2,1)S(1)}, bf16[2,64,1152]{2,1,0:T(8,128)(2,1)S(1)}, u32[]{:S(2)}, u32[]{:S(2)}) collective-permute-start(bf16[2,64,1152]{2,1,0:T(8,128)(2,1)S(1)} %get-tuple-element.43), channel_id=1, source_target_pairs={{0,4},{1,5},{2,6},{3,7},{4,8},{5,9},{6,10},{7,11},{8,12},{9,13},{1... | collective-permute-start | bytes 884744 | tf_op jit(solution)/shard_map/ppermute | solution.py:389
  97.9 46.2 %collective-permute-start.23 = (bf16[2,64,1152]{2,1,0:T(8,128)(2,1)S(1)}, bf16[2,64,1152]{2,1,0:T(8,128)(2,1)S(1)}, u32[]{:S(2)}, u32[]{:S(2)}) collective-permute-start(bf16[2,64,1152]{2,1,0:T(8,128)(2,1)S(1)} %get-tuple-element.44), channel_id=1, source_target_pairs={{0,6},{1,7},{2,4},{3,5},{4,10},{5,11},{6,8},{7,9},{8,14},{9,15},{1... | collective-permute-start | bytes 884744 | tf_op jit(solution)/shard_map/ppermute | solution.py:389
  97.9 46.3 %collective-permute-start.24 = (bf16[2,64,1152]{2,1,0:T(8,128)(2,1)S(1)}, bf16[2,64,1152]{2,1,0:T(8,128)(2,1)S(1)}, u32[]{:S(2)}, u32[]{:S(2)}) collective-permute-start(bf16[2,64,1152]{2,1,0:T(8,128)(2,1)S(1)} %get-tuple-element.45), channel_id=1, source_target_pairs={{0,8},{1,9},{4,12},{5,13},{8,16},{9,17},{12,20},{13,21},{16,24},{1... | collective-permute-start | bytes 884744 | tf_op jit(solution)/shard_map/ppermute | solution.py:389
  110.5 35.7 %collective-permute-start.25 = (bf16[2,64,1152]{2,1,0:T(8,128)(2,1)S(1)}, bf16[2,64,1152]{2,1,0:T(8,128)(2,1)S(1)}, u32[]{:S(2)}, u32[]{:S(2)}) collective-permute-start(bf16[2,64,1152]{2,1,0:T(8,128)(2,1)S(1)} %get-tuple-element.46), channel_id=1, source_target_pairs={{2,8},{3,9},{6,12},{7,13},{10,16},{11,17},{14,20},{15,21},{18,24},... | collective-permute-start | bytes 884744 | tf_op jit(solution)/shard_map/ppermute | solution.py:389
  141.1 9.8 %collective-permute-start.13 = (bf16[2,64,1152]{2,1,0:T(8,128)(2,1)S(1)}, bf16[2,64,1152]{2,1,0:T(8,128)(2,1)S(1)}, u32[]{:S(2)}, u32[]{:S(2)}) collective-permute-start(bf16[2,64,1152]{2,1,0:T(8,128)(2,1)S(1)} %get-tuple-element.32), channel_id=1, source_target_pairs={{0,2},{1,3},{2,0},{3,1},{4,6},{5,7},{6,4},{7,5},{8,10},{9,11},{10,... | collective-permute-start | bytes 884744 | tf_op jit(solution)/shard_map/ppermute | solution.py:389
  144.1 9.9 %collective-permute-start.14 = (bf16[2,64,1152]{2,1,0:T(8,128)(2,1)S(1)}, bf16[2,64,1152]{2,1,0:T(8,128)(2,1)S(1)}, u32[]{:S(2)}, u32[]{:S(2)}) collective-permute-start(bf16[2,64,1152]{2,1,0:T(8,128)(2,1)S(1)} %get-tuple-element.33), channel_id=1, source_target_pairs={{0,4},{1,5},{2,6},{3,7},{4,8},{5,9},{6,10},{7,11},{8,12},{9,13},{1... | collective-permute-start | bytes 884744 | tf_op jit(solution)/shard_map/ppermute | solution.py:389
  144.1 14.4 %collective-permute-start.15 = (bf16[2,64,1152]{2,1,0:T(8,128)(2,1)S(1)}, bf16[2,64,1152]{2,1,0:T(8,128)(2,1)S(1)}, u32[]{:S(2)}, u32[]{:S(2)}) collective-permute-start(bf16[2,64,1152]{2,1,0:T(8,128)(2,1)S(1)} %get-tuple-element.34), channel_id=1, source_target_pairs={{0,6},{1,7},{2,4},{3,5},{4,10},{5,11},{6,8},{7,9},{8,14},{9,15},{1... | collective-permute-start | bytes 884744 | tf_op jit(solution)/shard_map/ppermute | solution.py:389
  144.2 21.5 %collective-permute-start.16 = (bf16[2,64,1152]{2,1,0:T(8,128)(2,1)S(1)}, bf16[2,64,1152]{2,1,0:T(8,128)(2,1)S(1)}, u32[]{:S(2)}, u32[]{:S(2)}) collective-permute-start(bf16[2,64,1152]{2,1,0:T(8,128)(2,1)S(1)} %get-tuple-element.35), channel_id=1, source_target_pairs={{0,8},{1,9},{4,12},{5,13},{8,16},{9,17},{12,20},{13,21},{16,24},{1... | collective-permute-start | bytes 884744 | tf_op jit(solution)/shard_map/ppermute | solution.py:389
  146.1 19.6 %collective-permute-start.17 = (bf16[2,64,1152]{2,1,0:T(8,128)(2,1)S(1)}, bf16[2,64,1152]{2,1,0:T(8,128)(2,1)S(1)}, u32[]{:S(2)}, u32[]{:S(2)}) collective-permute-start(bf16[2,64,1152]{2,1,0:T(8,128)(2,1)S(1)} %get-tuple-element.36), channel_id=1, source_target_pairs={{2,8},{3,9},{6,12},{7,13},{10,16},{11,17},{14,20},{15,21},{18,24},... | collective-permute-start | bytes 884744 | tf_op jit(solution)/shard_map/ppermute | solution.py:389
  (4 other events, 3.7 us)
where the time goes:
time: 170 us; the launch traced here: 169 us
  Pallas kernels  64.9 us (38%)
  waiting for transfers between devices  54.1 us (32%)
  starting transfers between devices  32.9 us (19%)
  local copies, waits for them, and re-layouts  15.2 us (9%)
    pallas_call x2, Pallas kernels, prompt_call(): pl.pallas_call(partial(prompt_kernel, sub, members, links, cap, group_siz...  58.2 us
    ppermute x10, waiting for transfers between devices, to_prompt(): return lax.ppermute(value, AXES, pairs_of(s, i, False))  23.9 us
    ppermute x10, starting transfers between devices, to_prompt(): return lax.ppermute(value, AXES, pairs_of(s, i, False))  16 us
    ppermute x6, waiting for transfers between devices, cache_part(): return lax.ppermute(part, AXES, pairs)  15.3 us
    ppermute x10, waiting for transfers between devices, shards(): results.append(lax.ppermute(parts[n], AXES, pairs_of(s, i, True)))  14.9 us
    ppermute x10, starting transfers between devices, shards(): results.append(lax.ppermute(parts[n], AXES, pairs_of(s, i, True)))  10.6 us
    dynamic_slice x2, local copies, waits for them, and re-layouts, cache_slice(): return lax.dynamic_slice_in_dim(cache, other * HD, HD, 2)  8.03 us
    pallas_call x2, Pallas kernels, merge_call(): pl.pallas_call(partial(merge_kernel, sub, heads, h, links, cap, group_siz...  6.7 us
  transfers between devices with their start and end apart: 26, of which 11 were waited for; matrix products, arithmetic and copies ran while one was open for 6% of the time, Pallas kernels for 36%

commit v1 on v0

--- a/solution.py
+++ b/solution.py
@@ -21,21 +21,42 @@
 masked_score = -1e30
 
 
-def prompt_kernel(sub, members, links, cap, group_size, stage, info_ref, *refs):
+def prompt_kernel(sub, members, links, cap, group_size, stage, last, blocks, info_ref, *refs):
     count = len(links)
     kv_refs = refs[: sub * members]
     query_refs = refs[sub * members : sub * members + count]
-    out_refs = refs[sub * members + count : sub * members + 2 * count]
-    keys, values, asked, answers, sems, query_sems, out_sems = refs[sub * members + 2 * count :]
+    if last:
+        state_in = refs[sub * members + count]
+        out_refs = refs[sub * members + count + 1 : sub * members + 2 * count + 1]
+        keys, values, asked, kept, sems, query_sems, state_sem, answers, out_sems = refs[
+            sub * members + 2 * count + 1 :
+        ]
+    else:
+        state_out = refs[sub * members + count]
+        keys, values, asked, kept, sems, query_sems, state_sem = refs[sub * members + count + 1 :]
     tokens = kv_refs[0].shape[1]
     rows = asked.shape[1]
     width = group_size * HD
     factor = HD ** -0.5 * LOG2E
-    blocks = members * tokens // BLOCK
     per_piece = max(1, PIECE // rows)
     pieces = group_size // per_piece
     piece = per_piece * rows
 
+    def each_wanted(action):
+        def visit(c, carry):
+            @pl.when(info_ref[sub * (blocks + 1) + c] >= 0)
+            def _():
+                if last:
+                    action(pltpu.make_async_copy(state_in.at[c], kept.at[c], state_sem.at[c]))
+                else:
+                    action(pltpu.make_async_copy(kept.at[c], state_out.at[c], state_sem.at[c]))
+
+            return carry
+
+        lax.fori_loop(0, count * cap, visit, 0)
+
+    if last:
+        each_wanted(lambda copy: copy.start())
     copies = []
     for j in range(sub):
         for r in range(members):
@@ -58,6 +79,8 @@
         copies.append(copy)
     for copy in copies:
         copy.wait()
+    if last:
+        each_wanted(lambda copy: copy.wait())
 
     lane = lax.broadcasted_iota(jnp.int32, (rows, HD), 1)
 
@@ -105,13 +128,22 @@
                     result.append((new_peak, acc))
                 return tuple(result)
 
-            state = tuple(
-                (
-                    jnp.full((piece, 1), masked_score, jnp.float32),
-                    jnp.zeros((piece, 2 * HD), jnp.float32),
+            if last:
+                state = []
+                for a in range(pieces):
+                    whole = kept[c, a * piece : (a + 1) * piece, :]
+                    peak = whole[:, 2 * HD - 1 :]
+                    total = jnp.broadcast_to(whole[:, HD : HD + 1], (piece, HD))
+                    state.append((peak, jnp.concatenate([whole[:, :HD], total], axis=1)))
+                state = tuple(state)
+            else:
+                state = tuple(
+                    (
+                        jnp.full((piece, 1), masked_score, jnp.float32),
+                        jnp.zeros((piece, 2 * HD), jnp.float32),
+                    )
+                    for _ in range(pieces)
                 )
-                for _ in range(pieces)
-            )
             done = 0
             for gather in LADDER:
                 if blocks % gather:
@@ -126,6 +158,16 @@
             state = lax.fori_loop(
                 start, (length + chunk - 1) // chunk, partial(step, gather, True), state
             )
+            if not last:
+                side = lax.broadcasted_iota(jnp.int32, (piece, HD), 1)
+                for a in range(pieces):
+                    peak, acc = state[a]
+                    tail = jnp.where(side < HD // 2, acc[:, HD:], peak)
+                    kept[c, a * piece : (a + 1) * piece, :] = jnp.concatenate(
+                        [acc[:, :HD], tail], axis=1
+                    )
+                pltpu.make_async_copy(kept.at[c], state_out.at[c], state_sem.at[c]).start()
+                return
             stats = jnp.zeros((rows, HD), jnp.float32)
             for a in range(pieces):
                 peak, acc = state[a]
@@ -145,6 +187,9 @@
         return carry
 
     lax.fori_loop(0, count * cap, one, 0)
+    if not last:
+        each_wanted(lambda copy: copy.wait())
+        return
 
     copies = []
     for n in range(count):
@@ -155,38 +200,52 @@
         copy.wait()
 
 
-def prompt_call(sub, members, links, cap, group_size, stage, info, chunks, fetched):
+def prompt_call(sub, links, cap, group_size, stage, blocks, info, chunks, fetched, state):
+    last = state is not None
     rows = fetched[0].shape[1]
     tokens = chunks[0].shape[1]
+    members = len(chunks) // sub
     width = group_size * HD
     count = len(links)
     any_spec = pl.BlockSpec(memory_space=pl.ANY)
+    state_shape = (count * cap, rows * group_size, 2 * HD)
+    scratch = [
+        pltpu.VMEM((sub, members * tokens, HD), jnp.bfloat16),
+        pltpu.VMEM((sub, members * tokens, HD), jnp.bfloat16),
+        pltpu.VMEM((count * cap, rows, width), jnp.bfloat16),
+        pltpu.VMEM(state_shape, jnp.float32),
+        pltpu.SemaphoreType.DMA((sub, members, 2)),
+        pltpu.SemaphoreType.DMA((count,)),
+        pltpu.SemaphoreType.DMA((count * cap,)),
+    ]
+    operands = [*chunks, *fetched]
+    if last:
+        operands.append(state)
+        scratch += [
+            pltpu.VMEM((count * cap, rows, width + HD), jnp.bfloat16),
+            pltpu.SemaphoreType.DMA((count,)),
+        ]
+        out_shape = [jax.ShapeDtypeStruct((cap, rows, width + HD), jnp.bfloat16)] * count
+    else:
+        out_shape = [jax.ShapeDtypeStruct(state_shape, jnp.float32)]
     return pl.pallas_call(
-        partial(prompt_kernel, sub, members, links, cap, group_size, stage),
+        partial(prompt_kernel, sub, members, links, cap, group_size, stage, last, blocks),
         grid_spec=pltpu.PrefetchScalarGridSpec(
             num_scalar_prefetch=1,
             grid=(1,),
-            in_specs=[any_spec] * (len(chunks) + count),
-            out_specs=[any_spec] * count,
-            scratch_shapes=[
-                pltpu.VMEM((sub, members * tokens, HD), jnp.bfloat16),
-                pltpu.VMEM((sub, members * tokens, HD), jnp.bfloat16),
-                pltpu.VMEM((count * cap, rows, width), jnp.bfloat16),
-                pltpu.VMEM((count * cap, rows, width + HD), jnp.bfloat16),
-                pltpu.SemaphoreType.DMA((sub, members, 2)),
-                pltpu.SemaphoreType.DMA((count,)),
-                pltpu.SemaphoreType.DMA((count,)),
-            ],
+            in_specs=[any_spec] * len(operands),
+            out_specs=[any_spec] * len(out_shape),
+            scratch_shapes=scratch,
         ),
-        out_shape=[jax.ShapeDtypeStruct((cap, rows, width + HD), jnp.bfloat16)] * count,
-        compiler_params=pltpu.CompilerParams(vmem_limit_bytes=40 * 1024 * 1024),
+        out_shape=out_shape,
+        compiler_params=pltpu.CompilerParams(vmem_limit_bytes=48 * 1024 * 1024),
         cost_estimate=pl.CostEstimate(
             flops=cap * rows * width * members * tokens * 4 * sub,
             bytes_accessed=sub * members * tokens * HD * 4,
             transcendentals=cap * rows * group_size * members * tokens,
         ),
-        name="prompt_attention",
-    )(info, *chunks, *fetched)
+        name="prompt_last" if last else "prompt_first",
+    )(info, *operands)
 
 
 def merge_kernel(sub, heads, h, links, cap, group_size, info_ref, *refs):
@@ -358,28 +417,48 @@
         stage_chunks.append([cache_part(p, j, r) for p, (j, r) in zip(slices, seats_of)])
 
     per_member = tokens // BLOCK
-    rows_info = []
-    for j in range(sub):
-        row = metas[j]
-        table = row[cap + 1 :]
-        order = ((member - table // per_member) % members) * per_member + table % per_member
-        rows_info += [row[cap : cap + 1], order]
+    blocks = block_table.shape[1]
+    logical = jnp.arange(blocks, dtype=jnp.int32)
     wanted = []
     for n, (s, i) in enumerate(links):
-        decode = (s * sub + (seat ^ i))
+        decode = s * sub + (seat ^ i)
         prompt = decode - metas[n][:cap]
         here = (prompt >= 0) & (prompt < sub) & reaches(s, seat ^ i)
         wanted.append(jnp.where(here, prompt ^ seat, -1))
-    info = jnp.concatenate(rows_info + wanted).astype(jnp.int32)
+    infos = []
+    for last in (False, True):
+        rows_info = []
+        for j in range(sub):
+            length, table = metas[j][cap], metas[j][cap + 1 :]
+            turn = (member - table // per_member) % members
+            mine = (turn > 0) if last else (turn == 0)
+            place = (turn - 1 if last else turn) * per_member + table % per_member
+            live = jnp.clip(length - logical * BLOCK, 0, BLOCK)
+            rank = jnp.sum((mine[None, :] & (logical[None, :] < logical[:, None])), axis=1)
+            chosen = mine[:, None] & (rank[:, None] == logical[None, :])
+            rows_info.append(jnp.sum(jnp.where(mine, live, 0))[None])
+            rows_info.append(jnp.sum(jnp.where(chosen, place[:, None], 0), axis=0))
+        infos.append(jnp.concatenate(rows_info + wanted).astype(jnp.int32))
 
     own_offset = offsets.reshape(-1).astype(jnp.int32)
     served = jnp.where(own_offset <= seat, 0, (own_offset - seat + sub - 1) // sub)
     seats = jnp.stack([seat ^ i for i in range(sub)])
     merge_info = jnp.concatenate([served, seats]).astype(jnp.int32)
     output = None
+    near_chunks, far_chunks = [], []
+    for chunks in stage_chunks:
+        near_chunks.append([chunks[n] for n, (j, r) in enumerate(seats_of) if r == 0])
+        far_chunks.append([chunks[n] for n, (j, r) in enumerate(seats_of) if r > 0])
+    states = [
+        prompt_call(
+            sub, links, cap, group_size, h, blocks, infos[0], near_chunks[h], fetched, None
+        )[0]
+        for h in range(heads)
+    ]
+    states = lax.optimization_barrier(states)
     for h in range(heads):
         parts = prompt_call(
-            sub, members, links, cap, group_size, h, info, stage_chunks[h], fetched
+            sub, links, cap, group_size, h, blocks, infos[1], far_chunks[h], fetched, states[h]
         )
         results = []
         for n, (s, i) in enumerate(links):

time: 170 us -> 200 us (1.18)
  Pallas kernels: 64.9 us -> 108 us
  waiting for transfers between devices: 54.1 us -> 32 us
  other arithmetic: 0.99 us -> 6.02 us
  starting transfers between devices: 32.9 us -> 37.3 us
    pallas_call x2 -> x4, Pallas kernels: 58.2 us -> 101 us  [prompt_call(): pl.pallas_call(partial(prompt_kernel, sub, members, links, cap, group_siz...]
    ppermute x6, waiting for transfers between devices: 15.3 us -> 0.02 us  [cache_part(): return lax.ppermute(part, AXES, pairs)]
    ppermute x10, waiting for transfers between devices: 23.9 us -> 19.6 us  [to_prompt(): return lax.ppermute(value, AXES, pairs_of(s, i, False))]
    unnamed x20 -> x8, local copies, waits for them, and re-layouts: 3.72 us -> 1.24 us
    ppermute x10, waiting for transfers between devices: 14.9 us -> 12.5 us  [shards(): results.append(lax.ppermute(parts[n], AXES, pairs_of(s, i, True)))]
  transfers between devices with their start and end apart: 26 -> 26, of which waited for: 11 -> 6; matrix products, arithmetic and copies ran while one was open for 6% -> 9% of each run, Pallas kernels for 36% -> 53%
where the time goes in v1:
time: 200 us; the launch traced here: 199 us
  Pallas kernels  108 us (54%)
  starting transfers between devices  37.3 us (19%)
  waiting for transfers between devices  32 us (16%)
  local copies, waits for them, and re-layouts  14.1 us (7%)
  other arithmetic  6.02 us (3%)
    pallas_call x4, Pallas kernels, prompt_call(): pl.pallas_call(partial(prompt_kernel, sub, members, links, cap, group_siz...  101 us
    ppermute x10, waiting for transfers between devices, to_prompt(): return lax.ppermute(value, AXES, pairs_of(s, i, False))  19.6 us
    ppermute x10, starting transfers between devices, to_prompt(): return lax.ppermute(value, AXES, pairs_of(s, i, False))  17.8 us
    ppermute x10, waiting for transfers between devices, shards(): results.append(lax.ppermute(parts[n], AXES, pairs_of(s, i, True)))  12.5 us
    ppermute x10, starting transfers between devices, shards(): results.append(lax.ppermute(parts[n], AXES, pairs_of(s, i, True)))  11.2 us
    dynamic_slice x2, local copies, waits for them, and re-layouts, cache_slice(): return lax.dynamic_slice_in_dim(cache, other * HD, HD, 2)  8.67 us
    ppermute x6, starting transfers between devices, cache_part(): return lax.ppermute(part, AXES, pairs)  8.33 us
    pallas_call x2, Pallas kernels, merge_call(): pl.pallas_call(partial(merge_kernel, sub, heads, h, links, cap, group_siz...  6.69 us
  transfers between devices with their start and end apart: 26, of which 6 were waited for; matrix products, arithmetic and copies ran while one was open for 9% of the time, Pallas kernels for 53%

profile of v1, /device:TPU:18, one launch (start us, length us, event | category | flops | bytes accessed | tf_op | source)
XLA Modules:
  0.0 198.7 jit_solution(6812666185910719226)
XLA Ops:
  1.5 1.8 collective-permute-start.4
  3.3 2.4 %collective-permute-start.3 = (s32[1,35]{1,0:T(1,128)S(1)}, s32[1,35]{1,0:T(1,128)S(1)}, u32[]{:S(2)}, u32[]{:S(2)}) collective-permute-start(s32[1,35]{1,0:T(1,128)S(1)} %add_bitcast_fusion), channel_id=1, source_target_pairs={{8,0},{9,1},{12,4},{13,5},{16,8},{17,9},{20,12},{21,13},{24,16},{2... | collective-permute-start | bytes 428 | tf_op jit(solution)/shard_map/ppermute | solution.py:387
  5.9 4.7 %collective-permute-start = (s32[1,35]{1,0:T(1,128)S(1)}, s32[1,35]{1,0:T(1,128)S(1)}, u32[]{:S(2)}, u32[]{:S(2)}) collective-permute-start(s32[1,35]{1,0:T(1,128)S(1)} %add_bitcast_fusion), channel_id=1, source_target_pairs={{2,0},{3,1},{0,2},{1,3},{6,4},{7,5},{4,6},{5,7},{10,8},{11,9},{8,1... | collective-permute-start | bytes 428 | tf_op jit(solution)/shard_map/ppermute | solution.py:387
  12.8 4.3 %constant_dynamic-slice_fusion.6 = (bf16[2,2048,128]{2,1,0:T(8,128)(2,1)}, bf16[2,2048,128]{2,1,0:T(8,128)(2,1)}, bf16[2,2048,128]{2,1,0:T(8,128)(2,1)}, bf16[2,2048,128]{2,1,0:T(8,128)(2,1)}) fusion(bf16[2,2048,1024]{2,1,0:T(8,128)(2,1)} %param.6, s32[]{:T(128)S(6)} %select_n.261, s32[]{:T(128)S(6)} %select_n.260, s32[]{:T(128)S(6)} %select_n.259, ...), kind=kLoop, calls=%fused_computation.27 | loop fusion | bytes 8388624 | tf_op jit(solution)/shard_map/dynamic_slice | solution.py:399
  18.8 4.4 %constant_dynamic-slice_fusion.2 = (bf16[2,2048,128]{2,1,0:T(8,128)(2,1)}, bf16[2,2048,128]{2,1,0:T(8,128)(2,1)}, bf16[2,2048,128]{2,1,0:T(8,128)(2,1)}, bf16[2,2048,128]{2,1,0:T(8,128)(2,1)}) fusion(bf16[2,2048,1024]{2,1,0:T(8,128)(2,1)} %param.6, s32[]{:T(128)S(6)} %select_n.265, s32[]{:T(128)S(6)} %select_n.264, s32[]{:T(128)S(6)} %select_n.263, ...), kind=kLoop, calls=%fused_computation.23 | loop fusion | bytes 8388624 | tf_op jit(solution)/shard_map/dynamic_slice | solution.py:399
  23.1 2.0 collective-permute-start.11
  25.9 1.4 multiply_add_fusion
  28.6 2.4 %collective-permute-start.10 = (bf16[2,64,2048]{2,1,0:T(8,128)(2,1)S(1)}, bf16[2,64,2048]{2,1,0:T(8,128)(2,1)}, u32[]{:S(2)}, u32[]{:S(2)}) collective-permute-start(bf16[2,64,2048]{2,1,0:T(8,128)(2,1)S(1)} %get-tuple-element.74.refs_2_), channel_id=1, source_target_pairs={{8,0},{9,1},{12,4},{13,5},{16,8},{17,9},{20,12},{21,13},{24,16},{2... | collective-permute-start | bytes 1572872 | tf_op jit(solution)/shard_map/ppermute | solution.py:387
  31.0 1.1 collective-permute-done.11.refs_7_
  32.1 3.4 %collective-permute-start.8 = (bf16[2,64,2048]{2,1,0:T(8,128)(2,1)S(1)}, bf16[2,64,2048]{2,1,0:T(8,128)(2,1)}, u32[]{:S(2)}, u32[]{:S(2)}) collective-permute-start(bf16[2,64,2048]{2,1,0:T(8,128)(2,1)S(1)} %get-tuple-element.74.refs_2_), channel_id=1, source_target_pairs={{4,0},{5,1},{6,2},{7,3},{8,4},{9,5},{10,6},{11,7},{12,8},{13,9},{1... | collective-permute-start | bytes 1572872 | tf_op jit(solution)/shard_map/ppermute | solution.py:387
  35.6 1.4 concatenate.15.info_ref
  37.0 5.8 %collective-permute-done.9.refs_5_ = bf16[2,64,2048]{2,1,0:T(8,128)(2,1)S(1)} collective-permute-done((bf16[2,64,2048]{2,1,0:T(8,128)(2,1)}, bf16[2,64,2048]{2,1,0:T(8,128)(2,1)S(1)}, u32[]{:S(2)}, u32[]{:S(2)}) %collective-permute-start.9) | collective-permute-done | bytes 524320 | tf_op jit(solution)/shard_map/ppermute | solution.py:387
  42.8 5.1 %collective-permute-start.12 = (bf16[2,2048,128]{2,1,0:T(8,128)(2,1)}, bf16[2,2048,128]{2,1,0:T(8,128)(2,1)}, u32[]{:S(2)}, u32[]{:S(2)}) collective-permute-start(bf16[2,2048,128]{2,1,0:T(8,128)(2,1)} %get-tuple-element.32), channel_id=1, source_target_pairs={{0,2},{1,3},{2,0},{3,1},{4,6},{5,7},{6,4},{7,5},{8,10},{9,11},{10,... | collective-permute-start | bytes 3145736 | tf_op jit(solution)/shard_map/ppermute | solution.py:408
  47.9 1.6 collective-permute-start.19
  49.7 12.7 %collective-permute-done.8.refs_4_ = bf16[2,64,2048]{2,1,0:T(8,128)(2,1)} collective-permute-done((bf16[2,64,2048]{2,1,0:T(8,128)(2,1)S(1)}, bf16[2,64,2048]{2,1,0:T(8,128)(2,1)}, u32[]{:S(2)}, u32[]{:S(2)}) %collective-permute-start.8) | collective-permute-done | bytes 524320 | tf_op jit(solution)/shard_map/ppermute | solution.py:387
  62.4 1.5 collective-permute-start.5
  64.1 1.3 concatenate.14.info_ref
  65.4 1.2 copy-done.2
  66.6 20.2 %prompt_first.3.refs_8_ = f32[12,512,256]{2,1,0:T(8,128)} custom-call(s32[78]{0:T(128)S(1)} %concatenate.15.info_ref, bf16[2,2048,128]{2,1,0:T(8,128)(2,1)S(1)} %copy-done.2, bf16[2,2048,128]{2,1,0:T(8,128)(2,1)} %collective-permute-done.13.refs_1_, bf16[2,64,2048]{2,1,0:T(8,128)(2,1)S(1)} %get-tuple-element.74.refs_2_, ...), custom_call_target="tpu_custom_call" | custom-call | flops 2147483648 | bytes 2097152 | tf_op jit(solution)/shard_map/prompt_first/pallas_call | solution.py:231
  86.8 20.2 %prompt_first.2.refs_8_ = f32[12,512,256]{2,1,0:T(8,128)} custom-call(s32[78]{0:T(128)S(1)} %concatenate.15.info_ref, bf16[2,2048,128]{2,1,0:T(8,128)(2,1)S(1)} %copy-done.1, bf16[2,2048,128]{2,1,0:T(8,128)(2,1)} %collective-permute-done.12.refs_1_, bf16[2,64,2048]{2,1,0:T(8,128)(2,1)S(1)} %get-tuple-element.74.refs_2_, ...), custom_call_target="tpu_custom_call" | custom-call | flops 2147483648 | bytes 2097152 | tf_op jit(solution)/shard_map/prompt_first/pallas_call | solution.py:231
  107.1 30.5 %prompt_last.3 = (bf16[2,64,1152]{2,1,0:T(8,128)(2,1)S(1)}, bf16[2,64,1152]{2,1,0:T(8,128)(2,1)S(1)}, bf16[2,64,1152]{2,1,0:T(8,128)(2,1)S(1)}, bf16[2,64,1152]{...) custom-call(s32[78]{0:T(128)S(1)} %concatenate.14.info_ref, ...), custom_call_target="tpu_custom_call" | custom-call | flops 2147483648 | bytes 2097152 | tf_op jit(solution)/shard_map/prompt_last/pallas_call | solution.py:231
  138.4 1.9 collective-permute-start.24
  140.3 1.3 collective-permute-start.25
  141.6 30.3 %prompt_last.2 = (bf16[2,64,1152]{2,1,0:T(8,128)(2,1)S(1)}, bf16[2,64,1152]{2,1,0:T(8,128)(2,1)S(1)}, bf16[2,64,1152]{2,1,0:T(8,128)(2,1)S(1)}, bf16[2,64,1152]{...) custom-call(s32[78]{0:T(128)S(1)} %concatenate.14.info_ref, ...), custom_call_target="tpu_custom_call" | custom-call | flops 2147483648 | bytes 2097152 | tf_op jit(solution)/shard_map/prompt_last/pallas_call | solution.py:231
  171.9 3.7 %collective-permute-start.14 = (bf16[2,64,1152]{2,1,0:T(8,128)(2,1)S(1)}, bf16[2,64,1152]{2,1,0:T(8,128)(2,1)S(1)}, u32[]{:S(2)}, u32[]{:S(2)}) collective-permute-start(bf16[2,64,1152]{2,1,0:T(8,128)(2,1)S(1)} %get-tuple-element.37), channel_id=1, source_target_pairs={{0,2},{1,3},{2,0},{3,1},{4,6},{5,7},{6,4},{7,5},{8,10},{9,11},{10,... | collective-permute-start | bytes 884744 | tf_op jit(solution)/shard_map/ppermute | solution.py:468
  175.8 1.9 collective-permute-start.17
  177.7 1.5 collective-permute-start.18
  179.3 3.3 %merge.2.refs_8_ = bf16[2,64,4096]{2,1,0:T(8,128)(2,1)} custom-call(s32[4]{0:T(128)S(1)} %pad_add_fusion.info_ref, bf16[2,64,4096]{2,1,0:T(8,128)(2,1)S(1)} %copy-done, bf16[2,2,64,512]{3,2,1,0:T(8,128)(2,1)S(1)} %copy-done.3, bf16[2,64,1152]{2,1,0:T(8,128)(2,1)S(1)} %get-tuple-element.45.refs_2_, bf16[2,64,1152]{2,1,0:T(8,128)(2,1)S(1)} %collective-permute-done.21.refs_3_, ...), custom_call_target="tpu_custom_call" | custom-call | flops 67108864 | bytes 2097152 | tf_op jit(solution)/shard_map/merge/pallas_call | solution.py:323
  182.7 2.9 %collective-permute-done.15.refs_4_ = bf16[2,64,1152]{2,1,0:T(8,128)(2,1)S(1)} collective-permute-done((bf16[2,64,1152]{2,1,0:T(8,128)(2,1)S(1)}, bf16[2,64,1152]{2,1,0:T(8,128)(2,1)S(1)}, u32[]{:S(2)}, u32[]{:S(2)}) %collective-permute-start.15) | collective-permute-done | bytes 294944 | tf_op jit(solution)/shard_map/ppermute | solution.py:468
  185.6 4.5 %collective-permute-done.16.refs_5_ = bf16[2,64,1152]{2,1,0:T(8,128)(2,1)S(1)} collective-permute-done((bf16[2,64,1152]{2,1,0:T(8,128)(2,1)S(1)}, bf16[2,64,1152]{2,1,0:T(8,128)(2,1)S(1)}, u32[]{:S(2)}, u32[]{:S(2)}) %collective-permute-start.16) | collective-permute-done | bytes 294944 | tf_op jit(solution)/shard_map/ppermute | solution.py:468
  190.1 5.0 %collective-permute-done.17.refs_6_ = bf16[2,64,1152]{2,1,0:T(8,128)(2,1)S(1)} collective-permute-done((bf16[2,64,1152]{2,1,0:T(8,128)(2,1)S(1)}, bf16[2,64,1152]{2,1,0:T(8,128)(2,1)S(1)}, u32[]{:S(2)}, u32[]{:S(2)}) %collective-permute-start.17) | collective-permute-done | bytes 294944 | tf_op jit(solution)/shard_map/ppermute | solution.py:468
  195.1 3.4 %merge.3 = bf16[2,64,4096]{2,1,0:T(8,128)(2,1)} custom-call(s32[4]{0:T(128)S(1)} %pad_add_fusion.info_ref, bf16[2,64,4096]{2,1,0:T(8,128)(2,1)S(1)} %copy-done, bf16[2,2,64,512]{3,2,1,0:T(8,128)(2,1)S(1)} %copy-done.3, bf16[2,64,1152]{2,1,0:T(8,128)(2,1)S(1)} %get-tuple-element.36.refs_2_, ...), custom_call_target="tpu_custom_call", output_to_operand_aliasing={{}: (9, {})} | custom-call | flops 67108864 | bytes 2097152 | tf_op jit(solution)/shard_map/merge/pallas_call | solution.py:323
  (65 shorter events, 8.3 us)
Async XLA Ops:
  0.0 17.9 %copy-start = (bf16[2,64,4096]{2,1,0:T(8,128)(2,1)S(1)}, bf16[2,64,4096]{2,1,0:T(8,128)(2,1)}, u32[]{:S(2)}) copy-start(bf16[2,64,4096]{2,1,0:T(8,128)(2,1)} %refs_0_.3) | copy-start | bytes 3145732
  1.5 25.9 %collective-permute-start.4 = (s32[1,35]{1,0:T(1,128)S(1)}, s32[1,35]{1,0:T(1,128)S(1)}, u32[]{:S(2)}, u32[]{:S(2)}) collective-permute-start(s32[1,35]{1,0:T(1,128)S(1)} %add_bitcast_fusion), channel_id=1, source_target_pairs={{8,2},{9,3},{12,6},{13,7},{16,10},{17,11},{20,14},{21,15},{24,18},... | collective-permute-start | bytes 428 | tf_op jit(solution)/shard_map/ppermute | solution.py:387
  3.3 24.2 %collective-permute-start.3 = (s32[1,35]{1,0:T(1,128)S(1)}, s32[1,35]{1,0:T(1,128)S(1)}, u32[]{:S(2)}, u32[]{:S(2)}) collective-permute-start(s32[1,35]{1,0:T(1,128)S(1)} %add_bitcast_fusion), channel_id=1, source_target_pairs={{8,0},{9,1},{12,4},{13,5},{16,8},{17,9},{20,12},{21,13},{24,16},{2... | collective-permute-start | bytes 428 | tf_op jit(solution)/shard_map/ppermute | solution.py:387
  5.6 22.7 %collective-permute-start.2 = (s32[1,35]{1,0:T(1,128)S(1)}, s32[1,35]{1,0:T(1,128)S(1)}, u32[]{:S(2)}, u32[]{:S(2)}) collective-permute-start(s32[1,35]{1,0:T(1,128)S(1)} %add_bitcast_fusion), channel_id=1, source_target_pairs={{6,0},{7,1},{4,2},{5,3},{10,4},{11,5},{8,6},{9,7},{14,8},{15,9},{1... | collective-permute-start | bytes 428 | tf_op jit(solution)/shard_map/ppermute | solution.py:387
  5.7 22.9 %collective-permute-start.1 = (s32[1,35]{1,0:T(1,128)S(1)}, s32[1,35]{1,0:T(1,128)S(1)}, u32[]{:S(2)}, u32[]{:S(2)}) collective-permute-start(s32[1,35]{1,0:T(1,128)S(1)} %add_bitcast_fusion), channel_id=1, source_target_pairs={{4,0},{5,1},{6,2},{7,3},{8,4},{9,5},{10,6},{11,7},{12,8},{13,9},{1... | collective-permute-start | bytes 428 | tf_op jit(solution)/shard_map/ppermute | solution.py:387
  5.9 17.3 %collective-permute-start = (s32[1,35]{1,0:T(1,128)S(1)}, s32[1,35]{1,0:T(1,128)S(1)}, u32[]{:S(2)}, u32[]{:S(2)}) collective-permute-start(s32[1,35]{1,0:T(1,128)S(1)} %add_bitcast_fusion), channel_id=1, source_target_pairs={{2,0},{3,1},{0,2},{1,3},{6,4},{7,5},{4,6},{5,7},{10,8},{11,9},{8,1... | collective-permute-start | bytes 428 | tf_op jit(solution)/shard_map/ppermute | solution.py:387
  23.1 9.0 %collective-permute-start.11 = (bf16[2,64,2048]{2,1,0:T(8,128)(2,1)}, bf16[2,64,2048]{2,1,0:T(8,128)(2,1)S(1)}, u32[]{:S(2)}, u32[]{:S(2)}) collective-permute-start(bf16[2,64,2048]{2,1,0:T(8,128)(2,1)} %get-tuple-element.73), channel_id=1, source_target_pairs={{8,2},{9,3},{12,6},{13,7},{16,10},{17,11},{20,14},{21,15},{24,18},... | collective-permute-start | bytes 1572872 | tf_op jit(solution)/shard_map/ppermute | solution.py:387
  27.4 15.4 %collective-permute-start.9 = (bf16[2,64,2048]{2,1,0:T(8,128)(2,1)}, bf16[2,64,2048]{2,1,0:T(8,128)(2,1)S(1)}, u32[]{:S(2)}, u32[]{:S(2)}) collective-permute-start(bf16[2,64,2048]{2,1,0:T(8,128)(2,1)} %get-tuple-element.73), channel_id=1, source_target_pairs={{6,0},{7,1},{4,2},{5,3},{10,4},{11,5},{8,6},{9,7},{14,8},{15,9},{1... | collective-permute-start | bytes 1572872 | tf_op jit(solution)/shard_map/ppermute | solution.py:387
  27.5 20.4 %collective-permute-start.7 = (bf16[2,64,2048]{2,1,0:T(8,128)(2,1)}, bf16[2,64,2048]{2,1,0:T(8,128)(2,1)S(1)}, u32[]{:S(2)}, u32[]{:S(2)}) collective-permute-start(bf16[2,64,2048]{2,1,0:T(8,128)(2,1)} %get-tuple-element.73), channel_id=1, source_target_pairs={{2,0},{3,1},{0,2},{1,3},{6,4},{7,5},{4,6},{5,7},{10,8},{11,9},{8,1... | collective-permute-start | bytes 1572872 | tf_op jit(solution)/shard_map/ppermute | solution.py:387
  28.4 35.5 %collective-permute-start.13 = (bf16[2,2048,128]{2,1,0:T(8,128)(2,1)}, bf16[2,2048,128]{2,1,0:T(8,128)(2,1)}, u32[]{:S(2)}, u32[]{:S(2)}) collective-permute-start(bf16[2,2048,128]{2,1,0:T(8,128)(2,1)} %get-tuple-element.34), channel_id=1, source_target_pairs={{0,2},{1,3},{2,0},{3,1},{4,6},{5,7},{6,4},{7,5},{8,10},{9,11},{10,... | collective-permute-start | bytes 3145736 | tf_op jit(solution)/shard_map/ppermute | solution.py:408
  28.6 20.9 %collective-permute-start.10 = (bf16[2,64,2048]{2,1,0:T(8,128)(2,1)S(1)}, bf16[2,64,2048]{2,1,0:T(8,128)(2,1)}, u32[]{:S(2)}, u32[]{:S(2)}) collective-permute-start(bf16[2,64,2048]{2,1,0:T(8,128)(2,1)S(1)} %get-tuple-element.74.refs_2_), channel_id=1, source_target_pairs={{8,0},{9,1},{12,4},{13,5},{16,8},{17,9},{20,12},{21,13},{24,16},{2... | collective-permute-start | bytes 1572872 | tf_op jit(solution)/shard_map/ppermute | solution.py:387
  32.1 30.3 %collective-permute-start.8 = (bf16[2,64,2048]{2,1,0:T(8,128)(2,1)S(1)}, bf16[2,64,2048]{2,1,0:T(8,128)(2,1)}, u32[]{:S(2)}, u32[]{:S(2)}) collective-permute-start(bf16[2,64,2048]{2,1,0:T(8,128)(2,1)S(1)} %get-tuple-element.74.refs_2_), channel_id=1, source_target_pairs={{4,0},{5,1},{6,2},{7,3},{8,4},{9,5},{10,6},{11,7},{12,8},{13,9},{1... | collective-permute-start | bytes 1572872 | tf_op jit(solution)/shard_map/ppermute | solution.py:387
  42.8 44.0 %collective-permute-start.12 = (bf16[2,2048,128]{2,1,0:T(8,128)(2,1)}, bf16[2,2048,128]{2,1,0:T(8,128)(2,1)}, u32[]{:S(2)}, u32[]{:S(2)}) collective-permute-start(bf16[2,2048,128]{2,1,0:T(8,128)(2,1)} %get-tuple-element.32), channel_id=1, source_target_pairs={{0,2},{1,3},{2,0},{3,1},{4,6},{5,7},{6,4},{7,5},{8,10},{9,11},{10,... | collective-permute-start | bytes 3145736 | tf_op jit(solution)/shard_map/ppermute | solution.py:408
  47.9 59.1 %collective-permute-start.19 = (bf16[2,2048,128]{2,1,0:T(8,128)(2,1)}, bf16[2,2048,128]{2,1,0:T(8,128)(2,1)}, u32[]{:S(2)}, u32[]{:S(2)}) collective-permute-start(bf16[2,2048,128]{2,1,0:T(8,128)(2,1)} %get-tuple-element.42), channel_id=1, source_target_pairs={{0,1},{1,0},{2,3},{3,2},{4,5},{5,4},{6,7},{7,6},{8,9},{9,8},{10,11... | collective-permute-start | bytes 3145736 | tf_op jit(solution)/shard_map/ppermute | solution.py:408
  49.5 57.6 %collective-permute-start.20 = (bf16[2,2048,128]{2,1,0:T(8,128)(2,1)}, bf16[2,2048,128]{2,1,0:T(8,128)(2,1)}, u32[]{:S(2)}, u32[]{:S(2)}) collective-permute-start(bf16[2,2048,128]{2,1,0:T(8,128)(2,1)} %get-tuple-element.43), channel_id=1, source_target_pairs={{0,3},{1,2},{2,1},{3,0},{4,7},{5,6},{6,5},{7,4},{8,11},{9,10},{10,... | collective-permute-start | bytes 3145736 | tf_op jit(solution)/shard_map/ppermute | solution.py:408
  62.4 76.0 %collective-permute-start.5 = (bf16[2,2048,128]{2,1,0:T(8,128)(2,1)}, bf16[2,2048,128]{2,1,0:T(8,128)(2,1)}, u32[]{:S(2)}, u32[]{:S(2)}) collective-permute-start(bf16[2,2048,128]{2,1,0:T(8,128)(2,1)} %get-tuple-element.29), channel_id=1, source_target_pairs={{0,1},{1,0},{2,3},{3,2},{4,5},{5,4},{6,7},{7,6},{8,9},{9,8},{10,11... | collective-permute-start | bytes 3145736 | tf_op jit(solution)/shard_map/ppermute | solution.py:408
  63.9 76.4 %collective-permute-start.6 = (bf16[2,2048,128]{2,1,0:T(8,128)(2,1)}, bf16[2,2048,128]{2,1,0:T(8,128)(2,1)}, u32[]{:S(2)}, u32[]{:S(2)}) collective-permute-start(bf16[2,2048,128]{2,1,0:T(8,128)(2,1)} %get-tuple-element.30), channel_id=1, source_target_pairs={{0,3},{1,2},{2,1},{3,0},{4,7},{5,6},{6,5},{7,4},{8,11},{9,10},{10,... | collective-permute-start | bytes 3145736 | tf_op jit(solution)/shard_map/ppermute | solution.py:408
  65.4 1.2 copy-start.2
  66.6 20.2 %copy-start.1 = (bf16[2,2048,128]{2,1,0:T(8,128)(2,1)S(1)}, bf16[2,2048,128]{2,1,0:T(8,128)(2,1)}, u32[]{:S(2)}) copy-start(bf16[2,2048,128]{2,1,0:T(8,128)(2,1)} %get-tuple-element.31.refs_0_) | copy-start | bytes 3145732
  137.6 41.7 %copy-start.3 = (bf16[2,2,64,512]{3,2,1,0:T(8,128)(2,1)S(1)}, bf16[2,2,64,512]{3,2,1,0:T(8,128)(2,1)}, u32[]{:S(2)}) copy-start(bf16[2,2,64,512]{3,2,1,0:T(8,128)(2,1)} %refs_1_.3) | copy-start | bytes 786436
  137.6 34.3 %collective-permute-start.21 = (bf16[2,64,1152]{2,1,0:T(8,128)(2,1)S(1)}, bf16[2,64,1152]{2,1,0:T(8,128)(2,1)S(1)}, u32[]{:S(2)}, u32[]{:S(2)}) collective-permute-start(bf16[2,64,1152]{2,1,0:T(8,128)(2,1)S(1)} %get-tuple-element.46), channel_id=1, source_target_pairs={{0,2},{1,3},{2,0},{3,1},{4,6},{5,7},{6,4},{7,5},{8,10},{9,11},{10,... | collective-permute-start | bytes 884744 | tf_op jit(solution)/shard_map/ppermute | solution.py:468
  138.4 37.3 %collective-permute-start.22 = (bf16[2,64,1152]{2,1,0:T(8,128)(2,1)S(1)}, bf16[2,64,1152]{2,1,0:T(8,128)(2,1)S(1)}, u32[]{:S(2)}, u32[]{:S(2)}) collective-permute-start(bf16[2,64,1152]{2,1,0:T(8,128)(2,1)S(1)} %get-tuple-element.47), channel_id=1, source_target_pairs={{0,4},{1,5},{2,6},{3,7},{4,8},{5,9},{6,10},{7,11},{8,12},{9,13},{1... | collective-permute-start | bytes 884744 | tf_op jit(solution)/shard_map/ppermute | solution.py:468
  138.4 37.3 %collective-permute-start.23 = (bf16[2,64,1152]{2,1,0:T(8,128)(2,1)S(1)}, bf16[2,64,1152]{2,1,0:T(8,128)(2,1)S(1)}, u32[]{:S(2)}, u32[]{:S(2)}) collective-permute-start(bf16[2,64,1152]{2,1,0:T(8,128)(2,1)S(1)} %get-tuple-element.48), channel_id=1, source_target_pairs={{0,6},{1,7},{2,4},{3,5},{4,10},{5,11},{6,8},{7,9},{8,14},{9,15},{1... | collective-permute-start | bytes 884744 | tf_op jit(solution)/shard_map/ppermute | solution.py:468
  138.4 37.4 %collective-permute-start.24 = (bf16[2,64,1152]{2,1,0:T(8,128)(2,1)S(1)}, bf16[2,64,1152]{2,1,0:T(8,128)(2,1)S(1)}, u32[]{:S(2)}, u32[]{:S(2)}) collective-permute-start(bf16[2,64,1152]{2,1,0:T(8,128)(2,1)S(1)} %get-tuple-element.49), channel_id=1, source_target_pairs={{0,8},{1,9},{4,12},{5,13},{8,16},{9,17},{12,20},{13,21},{16,24},{1... | collective-permute-start | bytes 884744 | tf_op jit(solution)/shard_map/ppermute | solution.py:468
  140.3 37.4 %collective-permute-start.25 = (bf16[2,64,1152]{2,1,0:T(8,128)(2,1)S(1)}, bf16[2,64,1152]{2,1,0:T(8,128)(2,1)S(1)}, u32[]{:S(2)}, u32[]{:S(2)}) collective-permute-start(bf16[2,64,1152]{2,1,0:T(8,128)(2,1)S(1)} %get-tuple-element.50), channel_id=1, source_target_pairs={{2,8},{3,9},{6,12},{7,13},{10,16},{11,17},{14,20},{15,21},{18,24},... | collective-permute-start | bytes 884744 | tf_op jit(solution)/shard_map/ppermute | solution.py:468
  171.9 10.7 %collective-permute-start.14 = (bf16[2,64,1152]{2,1,0:T(8,128)(2,1)S(1)}, bf16[2,64,1152]{2,1,0:T(8,128)(2,1)S(1)}, u32[]{:S(2)}, u32[]{:S(2)}) collective-permute-start(bf16[2,64,1152]{2,1,0:T(8,128)(2,1)S(1)} %get-tuple-element.37), channel_id=1, source_target_pairs={{0,2},{1,3},{2,0},{3,1},{4,6},{5,7},{6,4},{7,5},{8,10},{9,11},{10,... | collective-permute-start | bytes 884744 | tf_op jit(solution)/shard_map/ppermute | solution.py:468
  175.7 9.9 %collective-permute-start.15 = (bf16[2,64,1152]{2,1,0:T(8,128)(2,1)S(1)}, bf16[2,64,1152]{2,1,0:T(8,128)(2,1)S(1)}, u32[]{:S(2)}, u32[]{:S(2)}) collective-permute-start(bf16[2,64,1152]{2,1,0:T(8,128)(2,1)S(1)} %get-tuple-element.38), channel_id=1, source_target_pairs={{0,4},{1,5},{2,6},{3,7},{4,8},{5,9},{6,10},{7,11},{8,12},{9,13},{1... | collective-permute-start | bytes 884744 | tf_op jit(solution)/shard_map/ppermute | solution.py:468
  175.7 14.4 %collective-permute-start.16 = (bf16[2,64,1152]{2,1,0:T(8,128)(2,1)S(1)}, bf16[2,64,1152]{2,1,0:T(8,128)(2,1)S(1)}, u32[]{:S(2)}, u32[]{:S(2)}) collective-permute-start(bf16[2,64,1152]{2,1,0:T(8,128)(2,1)S(1)} %get-tuple-element.39), channel_id=1, source_target_pairs={{0,6},{1,7},{2,4},{3,5},{4,10},{5,11},{6,8},{7,9},{8,14},{9,15},{1... | collective-permute-start | bytes 884744 | tf_op jit(solution)/shard_map/ppermute | solution.py:468
  175.8 19.3 %collective-permute-start.17 = (bf16[2,64,1152]{2,1,0:T(8,128)(2,1)S(1)}, bf16[2,64,1152]{2,1,0:T(8,128)(2,1)S(1)}, u32[]{:S(2)}, u32[]{:S(2)}) collective-permute-start(bf16[2,64,1152]{2,1,0:T(8,128)(2,1)S(1)} %get-tuple-element.40), channel_id=1, source_target_pairs={{0,8},{1,9},{4,12},{5,13},{8,16},{9,17},{12,20},{13,21},{16,24},{1... | collective-permute-start | bytes 884744 | tf_op jit(solution)/shard_map/ppermute | solution.py:468
  177.7 17.4 %collective-permute-start.18 = (bf16[2,64,1152]{2,1,0:T(8,128)(2,1)S(1)}, bf16[2,64,1152]{2,1,0:T(8,128)(2,1)S(1)}, u32[]{:S(2)}, u32[]{:S(2)}) collective-permute-start(bf16[2,64,1152]{2,1,0:T(8,128)(2,1)S(1)} %get-tuple-element.41), channel_id=1, source_target_pairs={{2,8},{3,9},{6,12},{7,13},{10,16},{11,17},{14,20},{15,21},{18,24},... | collective-permute-start | bytes 884744 | tf_op jit(solution)/shard_map/ppermute | solution.py:468

commit v2 on v1

--- a/solution.py
+++ b/solution.py
@@ -21,7 +21,7 @@
 masked_score = -1e30
 
 
-def prompt_kernel(sub, members, links, cap, group_size, stage, last, blocks, info_ref, *refs):
+def prompt_kernel(sub, members, links, cap, group_size, last, blocks, info_ref, *refs):
     count = len(links)
     kv_refs = refs[: sub * members]
     query_refs = refs[sub * members : sub * members + count]
@@ -36,7 +36,6 @@
         keys, values, asked, kept, sems, query_sems, state_sem = refs[sub * members + count + 1 :]
     tokens = kv_refs[0].shape[1]
     rows = asked.shape[1]
-    width = group_size * HD
     factor = HD ** -0.5 * LOG2E
     per_piece = max(1, PIECE // rows)
     pieces = group_size // per_piece
@@ -71,7 +70,7 @@
                 copies.append(copy)
     for n in range(count):
         copy = pltpu.make_async_copy(
-            query_refs[n].at[:, :, pl.ds(stage * width, width)],
+            query_refs[n],
             asked.at[pl.ds(n * cap, cap)],
             query_sems.at[n],
         )
@@ -200,7 +199,7 @@
         copy.wait()
 
 
-def prompt_call(sub, links, cap, group_size, stage, blocks, info, chunks, fetched, state):
+def prompt_call(sub, links, cap, group_size, blocks, info, chunks, fetched, state):
     last = state is not None
     rows = fetched[0].shape[1]
     tokens = chunks[0].shape[1]
@@ -229,7 +228,7 @@
     else:
         out_shape = [jax.ShapeDtypeStruct(state_shape, jnp.float32)]
     return pl.pallas_call(
-        partial(prompt_kernel, sub, members, links, cap, group_size, stage, last, blocks),
+        partial(prompt_kernel, sub, members, links, cap, group_size, last, blocks),
         grid_spec=pltpu.PrefetchScalarGridSpec(
             num_scalar_prefetch=1,
             grid=(1,),
@@ -391,8 +390,8 @@
     ).astype(jnp.int32)[None]
     metas = [to_prompt(lambda other: meta, s, i)[0] for s, i in links]
 
-    def query_part(other):
-        return lax.dynamic_slice_in_dim(queries, other * heads * width, heads * width, 2)
+    def query_part(h, other):
+        return lax.dynamic_slice_in_dim(queries, (other * heads + h) * width, width, 2)
 
     def cache_slice(cache, j, r, h):
         other = ((member + r) % members) * kv_local + (seat ^ j) * heads + h
@@ -407,7 +406,7 @@
         ]
         return lax.ppermute(part, AXES, pairs)
 
-    fetched = [to_prompt(query_part, s, i) for s, i in links]
+    fetched = [[to_prompt(partial(query_part, h), s, i) for s, i in links] for h in range(heads)]
     seats_of = [(j, r) for j in range(sub) for r in range(members)]
     stage_chunks = []
     cache = prompt_cache
@@ -451,14 +450,14 @@
         far_chunks.append([chunks[n] for n, (j, r) in enumerate(seats_of) if r > 0])
     states = [
         prompt_call(
-            sub, links, cap, group_size, h, blocks, infos[0], near_chunks[h], fetched, None
+            sub, links, cap, group_size, blocks, infos[0], near_chunks[h], fetched[h], None
         )[0]
         for h in range(heads)
     ]
     states = lax.optimization_barrier(states)
     for h in range(heads):
         parts = prompt_call(
-            sub, links, cap, group_size, h, blocks, infos[1], far_chunks[h], fetched, states[h]
+            sub, links, cap, group_size, blocks, infos[1], far_chunks[h], fetched[h], states[h]
         )
         results = []
         for n, (s, i) in enumerate(links):

time: 200 us -> 201 us (level)
  local copies, waits for them, and re-layouts: 14.1 us -> 19.8 us
  waiting for transfers between devices: 32 us -> 26.6 us
    ppermute x10 -> x15, waiting for transfers between devices: 19.6 us -> 12.4 us  [to_prompt(): return lax.ppermute(value, AXES, pairs_of(s, i, False))]
    unnamed x8 -> x38, local copies, waits for them, and re-layouts: 1.24 us -> 7.8 us
    ppermute x10 -> x15, starting transfers between devices: 17.8 us -> 21.7 us  [to_prompt(): return lax.ppermute(value, AXES, pairs_of(s, i, False))]
  transfers between devices with their start and end apart: 26 -> 31, of which waited for: 6 -> 8; matrix products, arithmetic and copies ran while one was open for 9% -> 9% of each run, Pallas kernels for 53% -> 52%
where the time goes in v2:
time: 201 us; the launch traced here: 199 us
  Pallas kernels  108 us (54%)
  starting transfers between devices  37.9 us (19%)
  waiting for transfers between devices  26.6 us (13%)
  local copies, waits for them, and re-layouts  19.8 us (10%)
  other arithmetic  5.9 us (3%)
    pallas_call x4, Pallas kernels, prompt_call(): pl.pallas_call(partial(prompt_kernel, sub, members, links, cap, group_siz...  101 us
    ppermute x15, starting transfers between devices, to_prompt(): return lax.ppermute(value, AXES, pairs_of(s, i, False))  21.7 us
    ppermute x10, waiting for transfers between devices, shards(): results.append(lax.ppermute(parts[n], AXES, pairs_of(s, i, True)))  12.4 us
    ppermute x15, waiting for transfers between devices, to_prompt(): return lax.ppermute(value, AXES, pairs_of(s, i, False))  12.4 us
    ppermute x10, starting transfers between devices, shards(): results.append(lax.ppermute(parts[n], AXES, pairs_of(s, i, True)))  9.57 us
    dynamic_slice x2, local copies, waits for them, and re-layouts, cache_slice(): return lax.dynamic_slice_in_dim(cache, other * HD, HD, 2)  7.96 us
    unnamed x38, local copies, waits for them, and re-layouts  7.8 us
    pallas_call x2, Pallas kernels, merge_call(): pl.pallas_call(partial(merge_kernel, sub, heads, h, links, cap, group_siz...  6.69 us
  transfers between devices with their start and end apart: 31, of which 8 were waited for; matrix products, arithmetic and copies ran while one was open for 9% of the time, Pallas kernels for 52%

profile of v2, /device:TPU:18, one launch (start us, length us, event | category | flops | bytes accessed | tf_op | source)
XLA Modules:
  0.0 199.5 jit_solution(9286161442813088352)
XLA Ops:
  1.5 1.8 collective-permute-start.4
  3.3 2.4 %collective-permute-start.3 = (s32[1,35]{1,0:T(1,128)S(1)}, s32[1,35]{1,0:T(1,128)S(1)}, u32[]{:S(2)}, u32[]{:S(2)}) collective-permute-start(s32[1,35]{1,0:T(1,128)S(1)} %add_bitcast_fusion), channel_id=1, source_target_pairs={{8,0},{9,1},{12,4},{13,5},{16,8},{17,9},{20,12},{21,13},{24,16},{2... | collective-permute-start | bytes 428 | tf_op jit(solution)/shard_map/ppermute | solution.py:386
  5.9 4.7 %collective-permute-start = (s32[1,35]{1,0:T(1,128)S(1)}, s32[1,35]{1,0:T(1,128)S(1)}, u32[]{:S(2)}, u32[]{:S(2)}) collective-permute-start(s32[1,35]{1,0:T(1,128)S(1)} %add_bitcast_fusion), channel_id=1, source_target_pairs={{2,0},{3,1},{0,2},{1,3},{6,4},{7,5},{4,6},{5,7},{10,8},{11,9},{8,1... | collective-permute-start | bytes 428 | tf_op jit(solution)/shard_map/ppermute | solution.py:386
  12.8 4.0 %constant_dynamic-slice_fusion.8 = (bf16[2,2048,128]{2,1,0:T(8,128)(2,1)}, bf16[2,2048,128]{2,1,0:T(8,128)(2,1)}, bf16[2,2048,128]{2,1,0:T(8,128)(2,1)}, bf16[2,2048,128]{2,1,0:T(8,128)(2,1)S(1)}) fusion(bf16[2,2048,1024]{2,1,0:T(8,128)(2,1)} %param.6, s32[]{:T(128)S(6)} %select_n.271, s32[]{:T(128)S(6)} %select_n.270, s32[]{:T(128)S(6)} %select_n.269, ...), kind=kLoop, calls=%fused_computation.29 | loop fusion | bytes 8388624 | tf_op jit(solution)/shard_map/dynamic_slice | solution.py:398
  18.3 4.0 %constant_dynamic-slice_fusion.4 = (bf16[2,2048,128]{2,1,0:T(8,128)(2,1)}, bf16[2,2048,128]{2,1,0:T(8,128)(2,1)}, bf16[2,2048,128]{2,1,0:T(8,128)(2,1)}, bf16[2,2048,128]{2,1,0:T(8,128)(2,1)S(1)}) fusion(bf16[2,2048,1024]{2,1,0:T(8,128)(2,1)} %param.6, s32[]{:T(128)S(6)} %select_n.275, s32[]{:T(128)S(6)} %select_n.274, s32[]{:T(128)S(6)} %select_n.273, ...), kind=kLoop, calls=%fused_computation.25 | loop fusion | bytes 8388624 | tf_op jit(solution)/shard_map/dynamic_slice | solution.py:398
  22.3 2.0 collective-permute-start.17
  25.2 1.3 multiply_add_fusion
  27.5 2.0 collective-permute-start.11
  31.5 4.5 %collective-permute-done.15.refs_5_ = bf16[2,64,1024]{2,1,0:T(8,128)(2,1)S(1)} collective-permute-done((bf16[2,64,1024]{2,1,0:T(8,128)(2,1)S(1)}, bf16[2,64,1024]{2,1,0:T(8,128)(2,1)S(1)}, u32[]{:S(2)}, u32[]{:S(2)}) %collective-permute-start.15) | collective-permute-done | bytes 262176 | tf_op jit(solution)/shard_map/ppermute | solution.py:386
  37.5 2.3 %collective-permute-start.16 = (bf16[2,64,1024]{2,1,0:T(8,128)(2,1)}, bf16[2,64,1024]{2,1,0:T(8,128)(2,1)S(1)}, u32[]{:S(2)}, u32[]{:S(2)}) collective-permute-start(bf16[2,64,1024]{2,1,0:T(8,128)(2,1)} %get-tuple-element.74.refs_2_), channel_id=1, source_target_pairs={{8,0},{9,1},{12,4},{13,5},{16,8},{17,9},{20,12},{21,13},{24,16},{2... | collective-permute-start | bytes 786440 | tf_op jit(solution)/shard_map/ppermute | solution.py:386
  42.4 2.3 %collective-permute-start.10 = (bf16[2,64,1024]{2,1,0:T(8,128)(2,1)S(1)}, bf16[2,64,1024]{2,1,0:T(8,128)(2,1)}, u32[]{:S(2)}, u32[]{:S(2)}) collective-permute-start(bf16[2,64,1024]{2,1,0:T(8,128)(2,1)S(1)} %get-tuple-element.76.refs_2_), channel_id=1, source_target_pairs={{8,0},{9,1},{12,4},{13,5},{16,8},{17,9},{20,12},{21,13},{24,16},{2... | collective-permute-start | bytes 786440 | tf_op jit(solution)/shard_map/ppermute | solution.py:386
  45.5 2.3 %collective-permute-start.12 = (bf16[2,2048,128]{2,1,0:T(8,128)(2,1)}, bf16[2,2048,128]{2,1,0:T(8,128)(2,1)}, u32[]{:S(2)}, u32[]{:S(2)}) collective-permute-start(bf16[2,2048,128]{2,1,0:T(8,128)(2,1)} %get-tuple-element.32), channel_id=1, source_target_pairs={{0,2},{1,3},{2,0},{3,1},{4,6},{5,7},{6,4},{7,5},{8,10},{9,11},{10,... | collective-permute-start | bytes 3145736 | tf_op jit(solution)/shard_map/ppermute | solution.py:407
  48.6 2.7 %collective-permute-start.8 = (bf16[2,64,1024]{2,1,0:T(8,128)(2,1)S(1)}, bf16[2,64,1024]{2,1,0:T(8,128)(2,1)}, u32[]{:S(2)}, u32[]{:S(2)}) collective-permute-start(bf16[2,64,1024]{2,1,0:T(8,128)(2,1)S(1)} %get-tuple-element.76.refs_2_), channel_id=1, source_target_pairs={{4,0},{5,1},{6,2},{7,3},{8,4},{9,5},{10,6},{11,7},{12,8},{13,9},{1... | collective-permute-start | bytes 786440 | tf_op jit(solution)/shard_map/ppermute | solution.py:386
  51.4 1.3 concatenate.15.info_ref
  53.6 1.5 collective-permute-start.24
  55.4 6.0 %collective-permute-done.8.refs_4_ = bf16[2,64,1024]{2,1,0:T(8,128)(2,1)} collective-permute-done((bf16[2,64,1024]{2,1,0:T(8,128)(2,1)S(1)}, bf16[2,64,1024]{2,1,0:T(8,128)(2,1)}, u32[]{:S(2)}, u32[]{:S(2)}) %collective-permute-start.8) | collective-permute-done | bytes 262176 | tf_op jit(solution)/shard_map/ppermute | solution.py:386
  61.4 1.5 collective-permute-start.5
  67.2 20.2 %prompt_first.3.refs_8_ = f32[12,512,256]{2,1,0:T(8,128)} custom-call(s32[78]{0:T(128)S(1)} %concatenate.15.info_ref, bf16[2,2048,128]{2,1,0:T(8,128)(2,1)S(1)} %get-tuple-element.33.refs_0_, bf16[2,2048,128]{2,1,0:T(8,128)(2,1)} %collective-permute-done.18.refs_1_, bf16[2,64,1024]{2,1,0:T(8,128)(2,1)S(1)} %get-tuple-element.76.refs_2_, ...), custom_call_target="tpu_custom_call" | custom-call | flops 2147483648 | bytes 2097152 | tf_op jit(solution)/shard_map/prompt_first/pallas_call | solution.py:230
  87.5 20.2 %prompt_first.2.refs_8_ = f32[12,512,256]{2,1,0:T(8,128)} custom-call(s32[78]{0:T(128)S(1)} %concatenate.15.info_ref, bf16[2,2048,128]{2,1,0:T(8,128)(2,1)S(1)} %get-tuple-element.31.refs_0_, bf16[2,2048,128]{2,1,0:T(8,128)(2,1)} %collective-permute-done.12.refs_1_, bf16[2,64,1024]{2,1,0:T(8,128)(2,1)} %get-tuple-element.74.refs_2_, ...), custom_call_target="tpu_custom_call" | custom-call | flops 2147483648 | bytes 2097152 | tf_op jit(solution)/shard_map/prompt_first/pallas_call | solution.py:230
  107.7 30.5 %prompt_last.3 = (bf16[2,64,1152]{2,1,0:T(8,128)(2,1)S(1)}, bf16[2,64,1152]{2,1,0:T(8,128)(2,1)S(1)}, bf16[2,64,1152]{2,1,0:T(8,128)(2,1)S(1)}, bf16[2,64,1152]{...) custom-call(s32[78]{0:T(128)S(1)} %concatenate.14.info_ref, ...), custom_call_target="tpu_custom_call" | custom-call | flops 2147483648 | bytes 2097152 | tf_op jit(solution)/shard_map/prompt_last/pallas_call | solution.py:230
  139.1 1.9 collective-permute-start.29
  141.0 1.8 collective-permute-done.6.refs_1_
  142.8 1.3 collective-permute-start.30
  144.1 30.3 %prompt_last.2 = (bf16[2,64,1152]{2,1,0:T(8,128)(2,1)S(1)}, bf16[2,64,1152]{2,1,0:T(8,128)(2,1)S(1)}, bf16[2,64,1152]{2,1,0:T(8,128)(2,1)S(1)}, bf16[2,64,1152]{...) custom-call(s32[78]{0:T(128)S(1)} %concatenate.14.info_ref, ...), custom_call_target="tpu_custom_call" | custom-call | flops 2147483648 | bytes 2097152 | tf_op jit(solution)/shard_map/prompt_last/pallas_call | solution.py:230
  174.5 2.0 %collective-permute-start.19 = (bf16[2,64,1152]{2,1,0:T(8,128)(2,1)S(1)}, bf16[2,64,1152]{2,1,0:T(8,128)(2,1)S(1)}, u32[]{:S(2)}, u32[]{:S(2)}) collective-permute-start(bf16[2,64,1152]{2,1,0:T(8,128)(2,1)S(1)} %get-tuple-element.37), channel_id=1, source_target_pairs={{0,2},{1,3},{2,0},{3,1},{4,6},{5,7},{6,4},{7,5},{8,10},{9,11},{10,... | collective-permute-start | bytes 884744 | tf_op jit(solution)/shard_map/ppermute | solution.py:467
  176.6 1.9 collective-permute-start.22
  178.5 1.6 collective-permute-start.23
  180.2 3.3 %merge.2.refs_8_ = bf16[2,64,4096]{2,1,0:T(8,128)(2,1)} custom-call(s32[4]{0:T(128)S(1)} %pad_add_fusion.info_ref, bf16[2,64,4096]{2,1,0:T(8,128)(2,1)S(1)} %copy-done, bf16[2,2,64,512]{3,2,1,0:T(8,128)(2,1)S(1)} %copy-done.18, bf16[2,64,1152]{2,1,0:T(8,128)(2,1)S(1)} %get-tuple-element.45.refs_2_, bf16[2,64,1152]{2,1,0:T(8,128)(2,1)S(1)} %collective-permute-done.26.refs_3_, ...), custom_call_target="tpu_custom_call" | custom-call | flops 67108864 | bytes 2097152 | tf_op jit(solution)/shard_map/merge/pallas_call | solution.py:322
  183.5 2.9 %collective-permute-done.20.refs_4_ = bf16[2,64,1152]{2,1,0:T(8,128)(2,1)S(1)} collective-permute-done((bf16[2,64,1152]{2,1,0:T(8,128)(2,1)S(1)}, bf16[2,64,1152]{2,1,0:T(8,128)(2,1)S(1)}, u32[]{:S(2)}, u32[]{:S(2)}) %collective-permute-start.20) | collective-permute-done | bytes 294944 | tf_op jit(solution)/shard_map/ppermute | solution.py:467
  186.4 4.5 %collective-permute-done.21.refs_5_ = bf16[2,64,1152]{2,1,0:T(8,128)(2,1)S(1)} collective-permute-done((bf16[2,64,1152]{2,1,0:T(8,128)(2,1)S(1)}, bf16[2,64,1152]{2,1,0:T(8,128)(2,1)S(1)}, u32[]{:S(2)}, u32[]{:S(2)}) %collective-permute-start.21) | collective-permute-done | bytes 294944 | tf_op jit(solution)/shard_map/ppermute | solution.py:467
  190.9 5.0 %collective-permute-done.22.refs_6_ = bf16[2,64,1152]{2,1,0:T(8,128)(2,1)S(1)} collective-permute-done((bf16[2,64,1152]{2,1,0:T(8,128)(2,1)S(1)}, bf16[2,64,1152]{2,1,0:T(8,128)(2,1)S(1)}, u32[]{:S(2)}, u32[]{:S(2)}) %collective-permute-start.22) | collective-permute-done | bytes 294944 | tf_op jit(solution)/shard_map/ppermute | solution.py:467
  195.9 3.4 %merge.3 = bf16[2,64,4096]{2,1,0:T(8,128)(2,1)} custom-call(s32[4]{0:T(128)S(1)} %pad_add_fusion.info_ref, bf16[2,64,4096]{2,1,0:T(8,128)(2,1)S(1)} %copy-done, bf16[2,2,64,512]{3,2,1,0:T(8,128)(2,1)S(1)} %copy-done.18, bf16[2,64,1152]{2,1,0:T(8,128)(2,1)S(1)} %get-tuple-element.36.refs_2_, ...), custom_call_target="tpu_custom_call", output_to_operand_aliasing={{}: (9, {})} | custom-call | flops 67108864 | bytes 2097152 | tf_op jit(solution)/shard_map/merge/pallas_call | solution.py:322
  (105 shorter events, 20.6 us)
Async XLA Ops:
  1.5 25.0 %collective-permute-start.4 = (s32[1,35]{1,0:T(1,128)S(1)}, s32[1,35]{1,0:T(1,128)S(1)}, u32[]{:S(2)}, u32[]{:S(2)}) collective-permute-start(s32[1,35]{1,0:T(1,128)S(1)} %add_bitcast_fusion), channel_id=1, source_target_pairs={{8,2},{9,3},{12,6},{13,7},{16,10},{17,11},{20,14},{21,15},{24,18},... | collective-permute-start | bytes 428 | tf_op jit(solution)/shard_map/ppermute | solution.py:386
  3.3 23.3 %collective-permute-start.3 = (s32[1,35]{1,0:T(1,128)S(1)}, s32[1,35]{1,0:T(1,128)S(1)}, u32[]{:S(2)}, u32[]{:S(2)}) collective-permute-start(s32[1,35]{1,0:T(1,128)S(1)} %add_bitcast_fusion), channel_id=1, source_target_pairs={{8,0},{9,1},{12,4},{13,5},{16,8},{17,9},{20,12},{21,13},{24,16},{2... | collective-permute-start | bytes 428 | tf_op jit(solution)/shard_map/ppermute | solution.py:386
  5.6 21.8 %collective-permute-start.2 = (s32[1,35]{1,0:T(1,128)S(1)}, s32[1,35]{1,0:T(1,128)S(1)}, u32[]{:S(2)}, u32[]{:S(2)}) collective-permute-start(s32[1,35]{1,0:T(1,128)S(1)} %add_bitcast_fusion), channel_id=1, source_target_pairs={{6,0},{7,1},{4,2},{5,3},{10,4},{11,5},{8,6},{9,7},{14,8},{15,9},{1... | collective-permute-start | bytes 428 | tf_op jit(solution)/shard_map/ppermute | solution.py:386
  5.7 23.8 %collective-permute-start.1 = (s32[1,35]{1,0:T(1,128)S(1)}, s32[1,35]{1,0:T(1,128)S(1)}, u32[]{:S(2)}, u32[]{:S(2)}) collective-permute-start(s32[1,35]{1,0:T(1,128)S(1)} %add_bitcast_fusion), channel_id=1, source_target_pairs={{4,0},{5,1},{6,2},{7,3},{8,4},{9,5},{10,6},{11,7},{12,8},{13,9},{1... | collective-permute-start | bytes 428 | tf_op jit(solution)/shard_map/ppermute | solution.py:386
  5.9 16.5 %collective-permute-start = (s32[1,35]{1,0:T(1,128)S(1)}, s32[1,35]{1,0:T(1,128)S(1)}, u32[]{:S(2)}, u32[]{:S(2)}) collective-permute-start(s32[1,35]{1,0:T(1,128)S(1)} %add_bitcast_fusion), channel_id=1, source_target_pairs={{2,0},{3,1},{0,2},{1,3},{6,4},{7,5},{4,6},{5,7},{10,8},{11,9},{8,1... | collective-permute-start | bytes 428 | tf_op jit(solution)/shard_map/ppermute | solution.py:386
  22.3 7.3 %collective-permute-start.17 = (bf16[2,64,1024]{2,1,0:T(8,128)(2,1)S(1)}, bf16[2,64,1024]{2,1,0:T(8,128)(2,1)S(1)}, u32[]{:S(2)}, u32[]{:S(2)}) collective-permute-start(bf16[2,64,1024]{2,1,0:T(8,128)(2,1)S(1)} %get-tuple-element.73), channel_id=1, source_target_pairs={{8,2},{9,3},{12,6},{13,7},{16,10},{17,11},{20,14},{21,15},{24,18},... | collective-permute-start | bytes 786440 | tf_op jit(solution)/shard_map/ppermute | solution.py:386
  26.5 9.6 %collective-permute-start.15 = (bf16[2,64,1024]{2,1,0:T(8,128)(2,1)S(1)}, bf16[2,64,1024]{2,1,0:T(8,128)(2,1)S(1)}, u32[]{:S(2)}, u32[]{:S(2)}) collective-permute-start(bf16[2,64,1024]{2,1,0:T(8,128)(2,1)S(1)} %get-tuple-element.73), channel_id=1, source_target_pairs={{6,0},{7,1},{4,2},{5,3},{10,4},{11,5},{8,6},{9,7},{14,8},{15,9},{1... | collective-permute-start | bytes 786440 | tf_op jit(solution)/shard_map/ppermute | solution.py:386
  26.6 10.2 %collective-permute-start.13 = (bf16[2,64,1024]{2,1,0:T(8,128)(2,1)S(1)}, bf16[2,64,1024]{2,1,0:T(8,128)(2,1)S(1)}, u32[]{:S(2)}, u32[]{:S(2)}) collective-permute-start(bf16[2,64,1024]{2,1,0:T(8,128)(2,1)S(1)} %get-tuple-element.73), channel_id=1, source_target_pairs={{2,0},{3,1},{0,2},{1,3},{6,4},{7,5},{4,6},{5,7},{10,8},{11,9},{8,1... | collective-permute-start | bytes 786440 | tf_op jit(solution)/shard_map/ppermute | solution.py:386
  27.5 12.4 %collective-permute-start.11 = (bf16[2,64,1024]{2,1,0:T(8,128)(2,1)S(1)}, bf16[2,64,1024]{2,1,0:T(8,128)(2,1)S(1)}, u32[]{:S(2)}, u32[]{:S(2)}) collective-permute-start(bf16[2,64,1024]{2,1,0:T(8,128)(2,1)S(1)} %get-tuple-element.75), channel_id=1, source_target_pairs={{8,2},{9,3},{12,6},{13,7},{16,10},{17,11},{20,14},{21,15},{24,18},... | collective-permute-start | bytes 786440 | tf_op jit(solution)/shard_map/ppermute | solution.py:386
  29.5 12.2 %collective-permute-start.9 = (bf16[2,64,1024]{2,1,0:T(8,128)(2,1)S(1)}, bf16[2,64,1024]{2,1,0:T(8,128)(2,1)S(1)}, u32[]{:S(2)}, u32[]{:S(2)}) collective-permute-start(bf16[2,64,1024]{2,1,0:T(8,128)(2,1)S(1)} %get-tuple-element.75), channel_id=1, source_target_pairs={{6,0},{7,1},{4,2},{5,3},{10,4},{11,5},{8,6},{9,7},{14,8},{15,9},{1... | collective-permute-start | bytes 786440 | tf_op jit(solution)/shard_map/ppermute | solution.py:386
  30.3 32.5 %collective-permute-start.18 = (bf16[2,2048,128]{2,1,0:T(8,128)(2,1)}, bf16[2,2048,128]{2,1,0:T(8,128)(2,1)}, u32[]{:S(2)}, u32[]{:S(2)}) collective-permute-start(bf16[2,2048,128]{2,1,0:T(8,128)(2,1)} %get-tuple-element.34), channel_id=1, source_target_pairs={{0,2},{1,3},{2,0},{3,1},{4,6},{5,7},{6,4},{7,5},{8,10},{9,11},{10,... | collective-permute-start | bytes 3145736 | tf_op jit(solution)/shard_map/ppermute | solution.py:407
  36.8 8.0 %collective-permute-start.7 = (bf16[2,64,1024]{2,1,0:T(8,128)(2,1)S(1)}, bf16[2,64,1024]{2,1,0:T(8,128)(2,1)S(1)}, u32[]{:S(2)}, u32[]{:S(2)}) collective-permute-start(bf16[2,64,1024]{2,1,0:T(8,128)(2,1)S(1)} %get-tuple-element.75), channel_id=1, source_target_pairs={{2,0},{3,1},{0,2},{1,3},{6,4},{7,5},{4,6},{5,7},{10,8},{11,9},{8,1... | collective-permute-start | bytes 786440 | tf_op jit(solution)/shard_map/ppermute | solution.py:386
  37.5 10.4 %collective-permute-start.16 = (bf16[2,64,1024]{2,1,0:T(8,128)(2,1)}, bf16[2,64,1024]{2,1,0:T(8,128)(2,1)S(1)}, u32[]{:S(2)}, u32[]{:S(2)}) collective-permute-start(bf16[2,64,1024]{2,1,0:T(8,128)(2,1)} %get-tuple-element.74.refs_2_), channel_id=1, source_target_pairs={{8,0},{9,1},{12,4},{13,5},{16,8},{17,9},{20,12},{21,13},{24,16},{2... | collective-permute-start | bytes 786440 | tf_op jit(solution)/shard_map/ppermute | solution.py:386
  40.5 13.1 %collective-permute-start.14 = (bf16[2,64,1024]{2,1,0:T(8,128)(2,1)}, bf16[2,64,1024]{2,1,0:T(8,128)(2,1)}, u32[]{:S(2)}, u32[]{:S(2)}) collective-permute-start(bf16[2,64,1024]{2,1,0:T(8,128)(2,1)} %get-tuple-element.74.refs_2_), channel_id=1, source_target_pairs={{4,0},{5,1},{6,2},{7,3},{8,4},{9,5},{10,6},{11,7},{12,8},{13,9},{1... | collective-permute-start | bytes 786440 | tf_op jit(solution)/shard_map/ppermute | solution.py:386
  42.4 12.8 %collective-permute-start.10 = (bf16[2,64,1024]{2,1,0:T(8,128)(2,1)S(1)}, bf16[2,64,1024]{2,1,0:T(8,128)(2,1)}, u32[]{:S(2)}, u32[]{:S(2)}) collective-permute-start(bf16[2,64,1024]{2,1,0:T(8,128)(2,1)S(1)} %get-tuple-element.76.refs_2_), channel_id=1, source_target_pairs={{8,0},{9,1},{12,4},{13,5},{16,8},{17,9},{20,12},{21,13},{24,16},{2... | collective-permute-start | bytes 786440 | tf_op jit(solution)/shard_map/ppermute | solution.py:386
  45.5 42.0 %collective-permute-start.12 = (bf16[2,2048,128]{2,1,0:T(8,128)(2,1)}, bf16[2,2048,128]{2,1,0:T(8,128)(2,1)}, u32[]{:S(2)}, u32[]{:S(2)}) collective-permute-start(bf16[2,2048,128]{2,1,0:T(8,128)(2,1)} %get-tuple-element.32), channel_id=1, source_target_pairs={{0,2},{1,3},{2,0},{3,1},{4,6},{5,7},{6,4},{7,5},{8,10},{9,11},{10,... | collective-permute-start | bytes 3145736 | tf_op jit(solution)/shard_map/ppermute | solution.py:407
  48.6 12.7 %collective-permute-start.8 = (bf16[2,64,1024]{2,1,0:T(8,128)(2,1)S(1)}, bf16[2,64,1024]{2,1,0:T(8,128)(2,1)}, u32[]{:S(2)}, u32[]{:S(2)}) collective-permute-start(bf16[2,64,1024]{2,1,0:T(8,128)(2,1)S(1)} %get-tuple-element.76.refs_2_), channel_id=1, source_target_pairs={{4,0},{5,1},{6,2},{7,3},{8,4},{9,5},{10,6},{11,7},{12,8},{13,9},{1... | collective-permute-start | bytes 786440 | tf_op jit(solution)/shard_map/ppermute | solution.py:386
  53.6 54.1 %collective-permute-start.24 = (bf16[2,2048,128]{2,1,0:T(8,128)(2,1)}, bf16[2,2048,128]{2,1,0:T(8,128)(2,1)}, u32[]{:S(2)}, u32[]{:S(2)}) collective-permute-start(bf16[2,2048,128]{2,1,0:T(8,128)(2,1)} %get-tuple-element.42), channel_id=1, source_target_pairs={{0,1},{1,0},{2,3},{3,2},{4,5},{5,4},{6,7},{7,6},{8,9},{9,8},{10,11... | collective-permute-start | bytes 3145736 | tf_op jit(solution)/shard_map/ppermute | solution.py:407
  55.2 52.6 %collective-permute-start.25 = (bf16[2,2048,128]{2,1,0:T(8,128)(2,1)}, bf16[2,2048,128]{2,1,0:T(8,128)(2,1)}, u32[]{:S(2)}, u32[]{:S(2)}) collective-permute-start(bf16[2,2048,128]{2,1,0:T(8,128)(2,1)} %get-tuple-element.43), channel_id=1, source_target_pairs={{0,3},{1,2},{2,1},{3,0},{4,7},{5,6},{6,5},{7,4},{8,11},{9,10},{10,... | collective-permute-start | bytes 3145736 | tf_op jit(solution)/shard_map/ppermute | solution.py:407
  61.4 77.7 %collective-permute-start.5 = (bf16[2,2048,128]{2,1,0:T(8,128)(2,1)}, bf16[2,2048,128]{2,1,0:T(8,128)(2,1)}, u32[]{:S(2)}, u32[]{:S(2)}) collective-permute-start(bf16[2,2048,128]{2,1,0:T(8,128)(2,1)} %get-tuple-element.29), channel_id=1, source_target_pairs={{0,1},{1,0},{2,3},{3,2},{4,5},{5,4},{6,7},{7,6},{8,9},{9,8},{10,11... | collective-permute-start | bytes 3145736 | tf_op jit(solution)/shard_map/ppermute | solution.py:407
  62.9 79.9 %collective-permute-start.6 = (bf16[2,2048,128]{2,1,0:T(8,128)(2,1)}, bf16[2,2048,128]{2,1,0:T(8,128)(2,1)}, u32[]{:S(2)}, u32[]{:S(2)}) collective-permute-start(bf16[2,2048,128]{2,1,0:T(8,128)(2,1)} %get-tuple-element.30), channel_id=1, source_target_pairs={{0,3},{1,2},{2,1},{3,0},{4,7},{5,6},{6,5},{7,4},{8,11},{9,10},{10,... | collective-permute-start | bytes 3145736 | tf_op jit(solution)/shard_map/ppermute | solution.py:407
  107.7 72.5 %copy-start.18 = (bf16[2,2,64,512]{3,2,1,0:T(8,128)(2,1)S(1)}, bf16[2,2,64,512]{3,2,1,0:T(8,128)(2,1)}, u32[]{:S(2)}) copy-start(bf16[2,2,64,512]{3,2,1,0:T(8,128)(2,1)} %refs_1_.3) | copy-start | bytes 786436
  138.3 36.2 %collective-permute-start.26 = (bf16[2,64,1152]{2,1,0:T(8,128)(2,1)S(1)}, bf16[2,64,1152]{2,1,0:T(8,128)(2,1)S(1)}, u32[]{:S(2)}, u32[]{:S(2)}) collective-permute-start(bf16[2,64,1152]{2,1,0:T(8,128)(2,1)S(1)} %get-tuple-element.46), channel_id=1, source_target_pairs={{0,2},{1,3},{2,0},{3,1},{4,6},{5,7},{6,4},{7,5},{8,10},{9,11},{10,... | collective-permute-start | bytes 884744 | tf_op jit(solution)/shard_map/ppermute | solution.py:467
  139.1 37.4 %collective-permute-start.27 = (bf16[2,64,1152]{2,1,0:T(8,128)(2,1)S(1)}, bf16[2,64,1152]{2,1,0:T(8,128)(2,1)S(1)}, u32[]{:S(2)}, u32[]{:S(2)}) collective-permute-start(bf16[2,64,1152]{2,1,0:T(8,128)(2,1)S(1)} %get-tuple-element.47), channel_id=1, source_target_pairs={{0,4},{1,5},{2,6},{3,7},{4,8},{5,9},{6,10},{7,11},{8,12},{9,13},{1... | collective-permute-start | bytes 884744 | tf_op jit(solution)/shard_map/ppermute | solution.py:467
  139.1 37.4 %collective-permute-start.28 = (bf16[2,64,1152]{2,1,0:T(8,128)(2,1)S(1)}, bf16[2,64,1152]{2,1,0:T(8,128)(2,1)S(1)}, u32[]{:S(2)}, u32[]{:S(2)}) collective-permute-start(bf16[2,64,1152]{2,1,0:T(8,128)(2,1)S(1)} %get-tuple-element.48), channel_id=1, source_target_pairs={{0,6},{1,7},{2,4},{3,5},{4,10},{5,11},{6,8},{7,9},{8,14},{9,15},{1... | collective-permute-start | bytes 884744 | tf_op jit(solution)/shard_map/ppermute | solution.py:467
  139.1 37.5 %collective-permute-start.29 = (bf16[2,64,1152]{2,1,0:T(8,128)(2,1)S(1)}, bf16[2,64,1152]{2,1,0:T(8,128)(2,1)S(1)}, u32[]{:S(2)}, u32[]{:S(2)}) collective-permute-start(bf16[2,64,1152]{2,1,0:T(8,128)(2,1)S(1)} %get-tuple-element.49), channel_id=1, source_target_pairs={{0,8},{1,9},{4,12},{5,13},{8,16},{9,17},{12,20},{13,21},{16,24},{1... | collective-permute-start | bytes 884744 | tf_op jit(solution)/shard_map/ppermute | solution.py:467
  142.8 35.7 %collective-permute-start.30 = (bf16[2,64,1152]{2,1,0:T(8,128)(2,1)S(1)}, bf16[2,64,1152]{2,1,0:T(8,128)(2,1)S(1)}, u32[]{:S(2)}, u32[]{:S(2)}) collective-permute-start(bf16[2,64,1152]{2,1,0:T(8,128)(2,1)S(1)} %get-tuple-element.50), channel_id=1, source_target_pairs={{2,8},{3,9},{6,12},{7,13},{10,16},{11,17},{14,20},{15,21},{18,24},... | collective-permute-start | bytes 884744 | tf_op jit(solution)/shard_map/ppermute | solution.py:467
  174.5 9.0 %collective-permute-start.19 = (bf16[2,64,1152]{2,1,0:T(8,128)(2,1)S(1)}, bf16[2,64,1152]{2,1,0:T(8,128)(2,1)S(1)}, u32[]{:S(2)}, u32[]{:S(2)}) collective-permute-start(bf16[2,64,1152]{2,1,0:T(8,128)(2,1)S(1)} %get-tuple-element.37), channel_id=1, source_target_pairs={{0,2},{1,3},{2,0},{3,1},{4,6},{5,7},{6,4},{7,5},{8,10},{9,11},{10,... | collective-permute-start | bytes 884744 | tf_op jit(solution)/shard_map/ppermute | solution.py:467
  176.5 9.9 %collective-permute-start.20 = (bf16[2,64,1152]{2,1,0:T(8,128)(2,1)S(1)}, bf16[2,64,1152]{2,1,0:T(8,128)(2,1)S(1)}, u32[]{:S(2)}, u32[]{:S(2)}) collective-permute-start(bf16[2,64,1152]{2,1,0:T(8,128)(2,1)S(1)} %get-tuple-element.38), channel_id=1, source_target_pairs={{0,4},{1,5},{2,6},{3,7},{4,8},{5,9},{6,10},{7,11},{8,12},{9,13},{1... | collective-permute-start | bytes 884744 | tf_op jit(solution)/shard_map/ppermute | solution.py:467
  176.5 14.4 %collective-permute-start.21 = (bf16[2,64,1152]{2,1,0:T(8,128)(2,1)S(1)}, bf16[2,64,1152]{2,1,0:T(8,128)(2,1)S(1)}, u32[]{:S(2)}, u32[]{:S(2)}) collective-permute-start(bf16[2,64,1152]{2,1,0:T(8,128)(2,1)S(1)} %get-tuple-element.39), channel_id=1, source_target_pairs={{0,6},{1,7},{2,4},{3,5},{4,10},{5,11},{6,8},{7,9},{8,14},{9,15},{1... | collective-permute-start | bytes 884744 | tf_op jit(solution)/shard_map/ppermute | solution.py:467
  176.6 19.3 %collective-permute-start.22 = (bf16[2,64,1152]{2,1,0:T(8,128)(2,1)S(1)}, bf16[2,64,1152]{2,1,0:T(8,128)(2,1)S(1)}, u32[]{:S(2)}, u32[]{:S(2)}) collective-permute-start(bf16[2,64,1152]{2,1,0:T(8,128)(2,1)S(1)} %get-tuple-element.40), channel_id=1, source_target_pairs={{0,8},{1,9},{4,12},{5,13},{8,16},{9,17},{12,20},{13,21},{16,24},{1... | collective-permute-start | bytes 884744 | tf_op jit(solution)/shard_map/ppermute | solution.py:467
  178.5 17.4 %collective-permute-start.23 = (bf16[2,64,1152]{2,1,0:T(8,128)(2,1)S(1)}, bf16[2,64,1152]{2,1,0:T(8,128)(2,1)S(1)}, u32[]{:S(2)}, u32[]{:S(2)}) collective-permute-start(bf16[2,64,1152]{2,1,0:T(8,128)(2,1)S(1)} %get-tuple-element.41), channel_id=1, source_target_pairs={{2,8},{3,9},{6,12},{7,13},{10,16},{11,17},{14,20},{15,21},{18,24},... | collective-permute-start | bytes 884744 | tf_op jit(solution)/shard_map/ppermute | solution.py:467
  (18 other events, 276.5 us)
